TPU v7x, 768 devices: a whole 4x8x12 slice. The times are simulated.
768 devices in a mesh: seq: 12 (over z), tensor: 64 (over x, y, core).
Axes of the slice: x: 4, y: 8, z: 12, core: 2. Of those that a mesh axis runs over, the one named last changes fastest.
Arguments:
- layer_inputs: bfloat16 [2304, 6144], P('seq'), may hold values from -16 to 16
- projection_matrices: bfloat16 [6144, 3, 6144], P(None, None, 'tensor'), may hold values from -0.21875 to 0.21875
- result_sensitivity: bfloat16 [2304, 6144], P('seq', 'tensor'), may hold values from -4.5 to 4.5
- channel_fading_rate: float32 [64], P('tensor'), may hold values from 8.680556e-06 to 0.03
- loss_events: int32 [4], replicated, may hold values from 0 to 2303
Outputs:
- input_grad: bfloat16 [6144, 2304], P('tensor', 'seq')
- weight_grad: bfloat16 [6144, 3, 6144], P('seq', None, 'tensor')
All inputs are finite; a program needn't handle non-finite values.
Results may differ from a plain program's by a relative error of at most 0.023.
Values may be sent and summed in bfloat16 or wider, within the bound.
No kernel may reach another device: no remote copies, remote signals or barrier semaphores. Data moves between devices by JAX's collectives and lax.ppermute only.
A program may use at most 64 MiB of HBM per device.

v0:
```python
import math

import jax
import jax.numpy as jnp
from jax import lax
from jax.sharding import PartitionSpec as P

DH = 96


DROP_LOGARITHM = 0.3
CLIP_RMS = 0.5
EXACT = lax.Precision.HIGHEST


def body(layer_inputs, projection_matrices, result_sensitivity, channel_fading_rate, loss_events):
    row_count = layer_inputs.shape[0]
    head_count = result_sensitivity.shape[1] // DH
    scale = DH ** (-0.5)
    proj = jnp.einsum(
        "td,dpe->pte", layer_inputs, projection_matrices, preferred_element_type=jnp.float32
    )

    def per_head(flat):
        return flat.reshape(row_count, head_count, DH).transpose(1, 0, 2).astype(jnp.float32)

    query = per_head((proj[0] * scale).astype(jnp.bfloat16))
    keys = per_head(proj[1].astype(jnp.bfloat16))
    values = per_head(proj[2].astype(jnp.bfloat16))
    grads_out = per_head(result_sensitivity)
    element_location = lax.axis_index("seq") * row_count + jnp.arange(row_count, dtype=jnp.int32)
    memory_loss_sites = jnp.sum(
        (loss_events[None, :] == element_location[:, None]).astype(jnp.float32), axis=1
    )
    logarithm_values = -(channel_fading_rate[:, None] + DROP_LOGARITHM * memory_loss_sites[None, :])
    cumul = jnp.cumsum(logarithm_values, axis=1)
    totals = cumul[:, -1]
    tail_w = jnp.exp(totals[:, None] - cumul)
    head_w = jnp.exp(cumul)
    fwd_state = jnp.einsum("nsf,nse->nfe", values * tail_w[..., None], keys, precision=EXACT)
    rev_state = jnp.einsum("nte,ntf->nef", query * head_w[..., None], grads_out, precision=EXACT)
    all_tot, all_fwd, all_rev = (
        lax.all_gather(totals[None].astype(jnp.bfloat16), "seq", axis=0, tiled=True).astype(
            jnp.float32
        ),
        lax.all_gather(fwd_state[None].astype(jnp.bfloat16), "seq", axis=0, tiled=True).astype(
            jnp.float32
        ),
        lax.all_gather(rev_state[None].astype(jnp.bfloat16), "seq", axis=0, tiled=True).astype(
            jnp.float32
        ),
    )
    index = lax.axis_index("seq")
    ends = jnp.cumsum(all_tot, axis=0)
    bases = ends - all_tot
    mine_end = lax.dynamic_index_in_dim(ends, index, 0, keepdims=False)
    mine_base = lax.dynamic_index_in_dim(bases, index, 0, keepdims=False)
    order = jnp.arange(all_tot.shape[0], dtype=jnp.int32)
    before = (order < index)[:, None]
    after = (order > index)[:, None]
    fwd_w = jnp.exp(jnp.where(before, mine_base[None, :] - ends, -jnp.inf))
    rev_w = jnp.exp(jnp.where(after, bases - mine_end[None, :], -jnp.inf))
    prefix = jnp.einsum("jn,jnfe->nfe", fwd_w, all_fwd, precision=EXACT)
    suffix = jnp.einsum("jn,jnef->nef", rev_w, all_rev, precision=EXACT)
    steps_idx = jnp.arange(row_count)
    later = (steps_idx[:, None] >= steps_idx[None, :])[None]
    weight = jnp.exp(jnp.where(later, cumul[:, :, None] - cumul[:, None, :], -jnp.inf))
    scores = jnp.einsum("nte,nse->nts", query, keys, precision=EXACT) * weight
    dscores = jnp.einsum("ntf,nsf->nts", grads_out, values, precision=EXACT) * weight
    dquery = jnp.einsum("nts,nse->nte", dscores, keys, precision=EXACT) + head_w[
        ..., None
    ] * jnp.einsum("ntf,nfe->nte", grads_out, prefix, precision=EXACT)
    dkey = jnp.einsum("nts,nte->nse", dscores, query, precision=EXACT) + tail_w[
        ..., None
    ] * jnp.einsum("nsf,nef->nse", values, suffix, precision=EXACT)
    dvalue = jnp.einsum("nts,ntf->nsf", scores, grads_out, precision=EXACT) + tail_w[
        ..., None
    ] * jnp.einsum("nse,nef->nsf", keys, suffix, precision=EXACT)
    stacked = jnp.stack([dquery * scale, dkey, dvalue]).astype(jnp.bfloat16)
    grads = stacked.transpose(0, 2, 1, 3).reshape(3, row_count, head_count * DH)
    piece = projection_matrices
    input_sum = lax.psum_scatter(
        jnp.einsum("rpe,pte->rt", piece, grads, preferred_element_type=jnp.float32),
        "tensor",
        scatter_dimension=0,
        tiled=True,
    )
    piece = layer_inputs
    summed = lax.psum_scatter(
        jnp.einsum("tr,pte->rpe", piece, grads, preferred_element_type=jnp.float32).astype(
            jnp.bfloat16
        ),
        "seq",
        scatter_dimension=0,
        tiled=True,
    ).astype(jnp.float32)
    square = lax.psum(jnp.sum(summed * summed), ("seq", "tensor"))
    entries = layer_inputs.shape[1] * 3 * head_count * DH * lax.axis_size("tensor")
    factor = jnp.minimum(1.0, CLIP_RMS * math.sqrt(entries) / jnp.sqrt(square + 1e-06))
    return (input_sum.astype(jnp.bfloat16), (summed * factor).astype(jnp.bfloat16))


def solution(mesh):
    return jax.shard_map(
        body,
        mesh=mesh,
        in_specs=(P("seq", None), P(None, None, "tensor"), P("seq", "tensor"), P("tensor"), P()),
        out_specs=(P("tensor", "seq"), P("seq", None, "tensor")),
        check_vma=False,
    )
```

profile of v0, /device:TPU:1, one launch (start us, length us, event | category | flops | bytes accessed | tf_op | source)
XLA Modules:
  0.0 468.0 jit_solution(15815188124012743535)
XLA Ops:
  7.2 0.0 copy-start
  7.2 0.0 reduce-scatter.7.cloned.1.call-start
  8.0 0.9 convert_reduce_fusion
  9.0 0.3 reduce-window.6
  9.3 0.2 slice_reduce_fusion
  9.5 0.2 reduce-window.9
  9.7 0.1 broadcast.119
  9.8 0.6 slice.34
  11.0 0.7 subtract_exponential_fusion
  11.7 0.0 copy-done
  11.7 0.0 copy-start.4
  11.7 2.8 fusion.65
  14.5 0.0 copy-start.5
  14.5 0.2 convolution_multiply_fusion
  14.7 0.0 copy-done.4
  14.7 0.2 fusion.7
  14.9 0.9 fusion.33
  15.8 1.0 fusion.42
  16.8 0.9 fusion.66
  17.7 0.0 copy-done.5
  17.7 0.8 convolution_convert_fusion.1
  18.5 1.3 dynamic-slice
  19.8 0.7 dynamic-update-slice
  20.5 31.2 %all-gather.1 = bf16[1152,96]{1,0:T(8,128)(2,1)} all-gather(bf16[96,96]{1,0:T(8,128)(2,1)} %convolution_convert_fusion.1), channel_id=3, replica_groups=mesh['seq'=12,'tensor'=64] {'seq'}, dimensions={0}, use_global_device_ids=true | all-gather | bytes 239616 | tf_op jit(solution)/shard_map/all_gather | solution.py:49
  51.6 15.4 %all-reduce.1 = bf16[12]{0:T(256)(128)(2,1)S(1)} all-reduce(bf16[12]{0:T(256)(128)(2,1)S(1)} %dynamic-update-slice), channel_id=1, replica_groups=mesh['seq'=12,'tensor'=64] {'seq'}, use_global_device_ids=true, to_apply=%add.1 | all-reduce | flops 12 | bytes 48
  67.0 0.0 copy-start.6
  67.0 0.5 copy-done.6
  67.5 0.2 reduce_window_sum.32
  67.7 0.7 fusion.61
  68.4 0.6 constant_dynamic-slice_fusion
  69.0 1.0 convolution_convert_fusion.2
  70.0 0.6 constant_dynamic-slice_fusion.1
  70.6 1.9 fusion.21
  72.5 1.2 fusion.16
  73.7 0.0 copy-start.1
  73.7 1.2 fusion.17
  74.9 0.0 copy-start.2
  75.0 17.4 %all-gather = bf16[1152,96]{1,0:T(8,128)(2,1)S(1)} all-gather(bf16[96,96]{1,0:T(8,128)(2,1)S(1)} %convolution_convert_fusion.2), channel_id=2, replica_groups=mesh['seq'=12,'tensor'=64] {'seq'}, dimensions={0}, use_global_device_ids=true | all-gather | bytes 239616 | tf_op jit(solution)/shard_map/all_gather | solution.py:46
  92.4 0.9 fusion.23
  93.2 1.1 fusion.18
  94.4 0.0 copy-done.1
  94.4 0.0 copy-done.2
  94.4 0.0 copy-start.3
  94.4 0.6 copy-done.3
  95.0 3.7 convolution_bitcast_fusion
  98.6 6.2 %copy.28 = f32[6144,192]{1,0:T(8,128)} copy(f32[6144,192]{0,1:T(8,128)} %convolution_bitcast_fusion) | data formatting | bytes 9437184
  104.9 0.0 reduce-scatter.7.cloned.1.call-update
  104.9 0.0 reduce-scatter.5.cloned.1.call-start
  104.9 4.7 %fusion = bf16[6144,3,96]{0,2,1:T(8,128)(2,1)} fusion(bf16[192,6144]{1,0:T(8,128)(2,1)} %param.5, bf16[1,192,96]{2,1,0:T(8,128)(2,1)} %copy-done.1, bf16[1,192,96]{2,1,0:T(8,128)(2,1)} %copy-done.2, bf16[1,192,96]{2,1,0:T(8,128)(2,1)} %copy-done.3), kind=kOutput, calls=%fused_computation.2 | convolution fusion | flops 681357312 | bytes 6008832 | tf_op jit(solution)/shard_map/tr,pte->rpe/dot_general | solution.py:90
  109.6 0.0 reduce-scatter.5.cloned.1.call-update
  109.7 166.3 %reduce-scatter.7.cloned.1.call-done = f32[96,192]{1,0:T(8,128)} async-done(((f32[6144,192]{1,0:T(8,128)}), f32[96,192]{1,0:T(8,128)}) %reduce-scatter.7.cloned.1.call-update) | async-done | bytes 73744
  276.0 1.6 copy.29
  277.6 64.8 %reduce-scatter.5.cloned.1.call-done = bf16[512,3,96]{0,2,1:T(8,128)(2,1)} async-done(((bf16[6144,3,96]{0,2,1:T(8,128)(2,1)}), bf16[512,3,96]{0,2,1:T(8,128)(2,1)}) %reduce-scatter.5.cloned.1.call-update) | async-done | bytes 294928 | tf_op jit(solution)/shard_map/reduce_scatter | solution.py:89
  342.4 1.8 fusion.19
  344.2 1.5 copy.20
  345.7 113.0 %psum.7 = f32[]{:T(128)} all-reduce(f32[]{:T(128)} %fusion.19), channel_id=1, replica_groups=mesh['seq'=12,'tensor'=64] {'seq','tensor'}, use_global_device_ids=true, to_apply=%region_7.8 | all-reduce | flops 1 | bytes 8 | tf_op jit(solution)/shard_map/psum | solution.py:97
  459.4 1.7 fusion.20
  (7 shorter events, 0.0 us)
Async XLA Ops:
  7.2 4.5 copy-start
  7.2 268.8 %reduce-scatter.7.cloned.1.call-start = ((), (), s32[]{:S(2)}) async-start(), calls=%async_computation.3 | async-start | bytes 6389760
  11.7 3.0 copy-start.4
  14.5 3.2 copy-start.5
  67.0 0.5 copy-start.6
  73.7 20.6 %copy-start.1 = (bf16[1,192,96]{2,1,0:T(8,128)(2,1)}, bf16[1,192,96]{2,1,0:T(8,128)(2,1)S(1)}, u32[]{:S(2)}) copy-start(bf16[1,192,96]{2,1,0:T(8,128)(2,1)S(1)} %fusion.16) | copy-start | bytes 110596
  74.9 19.4 %copy-start.2 = (bf16[1,192,96]{2,1,0:T(8,128)(2,1)}, bf16[1,192,96]{2,1,0:T(8,128)(2,1)S(1)}, u32[]{:S(2)}) copy-start(bf16[1,192,96]{2,1,0:T(8,128)(2,1)S(1)} %fusion.17) | copy-start | bytes 110596
  94.4 0.6 copy-start.3
  104.9 237.5 %reduce-scatter.5.cloned.1.call-start = ((), (), s32[]{:S(2)}) async-start(), calls=%async_computation.2 | async-start | bytes 3833856 | tf_op jit(solution)/shard_map/reduce_scatter | solution.py:89
Sparse Core Ops, SparseCore 0:
  105.0 170.8 reduce-scatter.6
  279.4 62.9 reduce-scatter.4
where the time goes:
time: 469 us; the launch traced here: 468 us
  waiting for transfers between devices  231 us (49%)
  blocking collectives  177 us (38%)
  matrix products  22.5 us (5%)
  between operations  16.4 us (3%)
  local copies, waits for them, and re-layouts  14.5 us (3%)
  other arithmetic  6.47 us (1%)
    unnamed x3, waiting for transfers between devices  166 us
    psum x1, blocking collectives, body(): square = lax.psum(jnp.sum(summed * summed), ('seq', 'tensor'))  113 us
    reduce_scatter x1, waiting for transfers between devices, body(): lax.psum_scatter(jnp.einsum('tr,pte->rpe', piece, grads, preferred_elemen...  64.8 us
    all_gather x1, blocking collectives, body(): lax.all_gather(rev_state[None].astype(jnp.bfloat16), 'seq', axis=0, tiled...  31.2 us
    all_gather x1, blocking collectives, body(): lax.all_gather(fwd_state[None].astype(jnp.bfloat16), 'seq', axis=0, tiled...  17.4 us
    unnamed x1, blocking collectives  15.4 us
    unnamed x20, local copies, waits for them, and re-layouts  12.4 us
  transfers between devices with their start and end apart: 2, of which 2 were waited for; matrix products, arithmetic and copies ran while one was open for 1% of the time, Pallas kernels for 0%

commit v1 on v0

v1 whole, which is shorter than its diff:
```python
import math

import jax
import jax.numpy as jnp
from jax import lax
from jax.sharding import Mesh, PartitionSpec as P

DH = 96
N_SEQ = 12
NX, NY, NC = 4, 8, 2

DROP_LOGARITHM = 0.3
CLIP_RMS = 0.5
EXACT = lax.Precision.HIGHEST
F32 = jnp.float32
BF16 = jnp.bfloat16
TENSOR = ("x", "y", "core")


def body(layer_inputs, projection_matrices, result_sensitivity, channel_fading_rate, loss_events):
    row_count, width = layer_inputs.shape
    scale = DH ** (-0.5)
    me = lax.axis_index("seq")
    proj = jnp.einsum("td,dpe->pte", layer_inputs, projection_matrices, preferred_element_type=F32)
    query = (proj[0] * scale).astype(BF16)
    keys = proj[1].astype(BF16)
    values = proj[2].astype(BF16)
    rate = channel_fading_rate[0]

    steps = jnp.arange(row_count, dtype=jnp.int32)
    place = loss_events - me * row_count
    seen = jnp.sum(((place[None, :] <= steps[:, None]) & (place[None, :] >= 0)).astype(F32), axis=1)
    cumul = -(rate * (steps + 1).astype(F32) + DROP_LOGARITHM * seen)
    shards = jnp.arange(N_SEQ, dtype=jnp.int32)
    events_of = jnp.sum((loss_events[None, :] // row_count == shards[:, None]).astype(F32), axis=1)
    totals = -(rate * row_count + DROP_LOGARITHM * events_of)
    mine_total = jnp.sum(jnp.where(shards == me, totals, 0.0))
    low = jnp.minimum(shards, me)[:, None]
    high = jnp.maximum(shards, me)[:, None]
    between = (shards[None, :] > low) & (shards[None, :] < high)
    hop_w = jnp.exp(jnp.sum(jnp.where(between, totals[None, :], 0.0), axis=1))
    tail_w = jnp.exp(mine_total - cumul)
    head_w = jnp.exp(cumul)

    q32, k32, v32, o32 = (a.astype(F32) for a in (query, keys, values, result_sensitivity))
    fwd_state = jnp.einsum("sf,se->fe", v32 * tail_w[:, None], k32, precision=EXACT)
    rev_state = jnp.einsum("te,tf->ef", q32 * head_w[:, None], o32, precision=EXACT)
    to_later = (shards > me)[:, None, None]
    to_send = hop_w[:, None, None] * jnp.where(to_later, fwd_state[None], rev_state[None])
    got = lax.all_to_all(to_send.astype(BF16), "seq", 0, 0, tiled=True).astype(F32)
    prefix = jnp.sum(jnp.where((shards < me)[:, None, None], got, 0.0), axis=0)
    suffix = jnp.sum(jnp.where((shards > me)[:, None, None], got, 0.0), axis=0)

    later = steps[:, None] >= steps[None, :]
    weight = jnp.exp(jnp.where(later, cumul[:, None] - cumul[None, :], -jnp.inf))
    scores = jnp.einsum("te,se->ts", query, keys, preferred_element_type=F32) * weight
    dscores = jnp.einsum("tf,sf->ts", result_sensitivity, values, preferred_element_type=F32) * weight
    dquery = jnp.einsum("ts,se->te", dscores, k32, precision=EXACT) + head_w[:, None] * jnp.einsum(
        "tf,fe->te", o32, prefix, precision=EXACT
    )
    dkey = jnp.einsum("ts,te->se", dscores, q32, precision=EXACT) + tail_w[:, None] * jnp.einsum(
        "sf,ef->se", v32, suffix, precision=EXACT
    )
    dvalue = jnp.einsum("ts,tf->sf", scores, o32, precision=EXACT) + tail_w[:, None] * jnp.einsum(
        "se,ef->sf", k32, suffix, precision=EXACT
    )
    grads = jnp.stack([dquery * scale, dkey, dvalue]).astype(BF16)

    terms = jnp.einsum("tr,pte->rpe", layer_inputs, grads, preferred_element_type=F32).astype(BF16)
    summed = lax.psum_scatter(terms, "seq", scatter_dimension=0, tiled=True)

    part = jnp.einsum("rpe,pte->rt", projection_matrices, grads, preferred_element_type=F32)
    part = part.reshape(NX, NY, NC, width // (NX * NY * NC), row_count)
    core = lax.axis_index("core")
    keep = lax.dynamic_index_in_dim(part, core, 2, keepdims=False)
    give = lax.dynamic_index_in_dim(part, 1 - core, 2, keepdims=False).astype(BF16)
    taken = lax.ppermute(give, "core", [(0, 1), (1, 0)])
    part = (keep + taken.astype(F32)).astype(BF16)
    part = lax.all_to_all(part, "x", 0, 0, tiled=True)
    part = jnp.sum(part.astype(F32), axis=0).astype(BF16)
    part = lax.all_to_all(part, "y", 0, 0, tiled=True)
    input_grad = jnp.sum(part.astype(F32), axis=0).astype(BF16)

    summed, input_grad = lax.optimization_barrier((summed, input_grad))
    summed = summed.astype(F32)
    square = jnp.sum(summed * summed)
    spread = jnp.broadcast_to(square, (NX * NY * NC, 128))
    square = jnp.sum(lax.all_to_all(spread, TENSOR, 0, 0, tiled=True)[:, :1])
    spread = jnp.broadcast_to(square, (N_SEQ, 8, 128))
    square = jnp.sum(lax.all_to_all(spread, "seq", 0, 0, tiled=True)[:, :1, :1])
    entries = width * 3 * DH * (NX * NY * NC)
    factor = jnp.minimum(1.0, CLIP_RMS * math.sqrt(entries) / jnp.sqrt(square + 1e-06))
    return (input_grad, (summed * factor).astype(BF16))


def solution(mesh):
    fine = Mesh(mesh.devices.reshape(N_SEQ, NX, NY, NC), ("seq",) + TENSOR)
    return jax.shard_map(
        body,
        mesh=fine,
        in_specs=(P("seq", None), P(None, None, TENSOR), P("seq", TENSOR), P(TENSOR), P()),
        out_specs=(P(TENSOR, "seq"), P("seq", None, TENSOR)),
        check_vma=False,
    )
```

time: 469 us -> 206 us (0.44)
  waiting for transfers between devices: 231 us -> 7.61 us
  blocking collectives: 177 us -> 72.1 us
  local copies, waits for them, and re-layouts: 14.5 us -> 46.4 us
  starting transfers between devices: 0.08 us -> 20.6 us
  other arithmetic: 6.47 us -> 18.4 us
    unnamed x3 -> x1, waiting for transfers between devices: 166 us -> 0.02 us
    psum x1 -> x0, blocking collectives: 113 us -> none  [body(): square = lax.psum(jnp.sum(summed * summed), ('seq', 'tensor'))]
    all_to_all x0 -> x4, blocking collectives: none -> 72.1 us  [the longest x1 24.5 us: body(): part = lax.all_to_all(part, 'x', 0, 0, tiled=True)]
    reduce_scatter x1, waiting for transfers between devices: 64.8 us -> 0.01 us  [body(): summed = lax.psum_scatter(terms, 'seq', scatter_dimension=0, tiled=True)]
    all_gather x2 -> x0, blocking collectives: 48.6 us -> none  [the longest x1 31.2 us: body(): lax.all_gather(rev_state[None].astype(jnp.bfloat16), 'seq', axis=0, tiled...]
    dynamic_slice x2 -> x3, local copies, waits for them, and re-layouts: 1.16 us -> 24.6 us  [the longest x2 16.7 us: body(): keep = lax.dynamic_index_in_dim(part, core, 2, keepdims=False)]
    all_to_all x0 -> x1, starting transfers between devices: none -> 15.7 us  [body(): lax.all_to_all(to_send.astype(BF16), 'seq', 0, 0, tiled=True).astype(F32)]
    unnamed x1 -> x0, blocking collectives: 15.4 us -> none
  transfers between devices with their start and end apart: 2 -> 3, of which waited for: 2 -> 1; matrix products, arithmetic and copies ran while one was open for 1% -> 31% of each run, Pallas kernels for 0% -> 0%
where the time goes in v1:
time: 206 us; the launch traced here: 204 us
  blocking collectives  72.1 us (35%)
  local copies, waits for them, and re-layouts  46.4 us (23%)
  matrix products  23.5 us (11%)
  starting transfers between devices  20.6 us (10%)
  other arithmetic  18.4 us (9%)
  between operations  15.6 us (8%)
  waiting for transfers between devices  7.61 us (4%)
    all_to_all x1, blocking collectives, body(): part = lax.all_to_all(part, 'x', 0, 0, tiled=True)  24.5 us
    all_to_all x1, blocking collectives, body(): part = lax.all_to_all(part, 'y', 0, 0, tiled=True)  20.1 us
    dynamic_slice x2, local copies, waits for them, and re-layouts, body(): keep = lax.dynamic_index_in_dim(part, core, 2, keepdims=False)  16.7 us
    all_to_all x1, starting transfers between devices, body(): lax.all_to_all(to_send.astype(BF16), 'seq', 0, 0, tiled=True).astype(F32)  15.7 us
    all_to_all x1, blocking collectives, body(): square = jnp.sum(lax.all_to_all(spread, TENSOR, 0, 0, tiled=True)[:, :1])  15.1 us
    all_to_all x1, blocking collectives, body(): square = jnp.sum(lax.all_to_all(spread, 'seq', 0, 0, tiled=True)[:, :1, :1])  12.5 us
    reshape x1, local copies, waits for them, and re-layouts, body(): part = part.reshape(NX, NY, NC, width // (NX * NY * NC), row_count)  10.8 us
    unnamed x13, local copies, waits for them, and re-layouts  9.66 us
  transfers between devices with their start and end apart: 3, of which 1 were waited for; matrix products, arithmetic and copies ran while one was open for 31% of the time, Pallas kernels for 0%

profile of v1, /device:TPU:1, one launch (start us, length us, event | category | flops | bytes accessed | tf_op | source)
XLA Modules:
  0.0 204.2 jit_solution(12636472747861755326)
XLA Ops:
  7.2 0.0 copy-start
  7.2 0.6 iota_maximum_fusion
  7.8 1.0 and_select_fusion
  8.8 0.7 broadcast_compare_fusion
  10.1 0.1 convert_reduce_fusion.1
  10.2 0.1 convert_reduce_fusion
  10.3 0.6 fusion.40
  10.9 0.7 subtract_exponential_fusion
  11.5 0.9 select_reduce_fusion
  12.4 0.0 copy-done
  12.4 0.0 copy-start.5
  12.4 2.8 %fusion.5 = f32[3,192,96]{1,2,0:T(8,128)S(1)} fusion(bf16[6144,3,96]{0,2,1:T(8,128)(2,1)S(1)} %copy-done, bf16[192,6144]{1,0:T(8,128)(2,1)} %param.5), kind=kOutput, calls=%fused_computation.9 | convolution fusion | flops 679477248 | bytes 6119424 | tf_op jit(solution)/shard_map/td,dpe->pte/dot_general | solution.py:24
  15.2 0.0 copy-start.1
  15.2 0.2 fusion.25
  15.4 0.5 copy-done.1
  15.9 0.0 copy-done.5
  15.9 0.2 fusion.27
  16.1 0.9 multiply_convert_fusion
  17.0 15.7 %all-to-all-start = ((bf16[12,96,96]{2,1,0:T(8,128)(2,1)}), bf16[12,96,96]{2,1,0:T(8,128)(2,1)}, u32[]{:S(2)}, u32[]{:S(2)}) async-start(bf16[12,96,96]{2,1,0:T(8,128)(2,1)} %multiply_convert_fusion), calls=%async_computation | async-start | bytes 589824 | tf_op jit(solution)/shard_map/all_to_all | solution.py:50
  32.7 0.0 reduce-scatter.2.cloned.1.call-start
  32.8 1.1 fusion.8
  33.9 1.2 convolution_multiply_fusion
  35.1 1.7 fusion.52
  36.7 1.9 fusion.50
  38.6 1.8 fusion.44
  40.4 7.6 %all-to-all-done = bf16[12,96,96]{2,1,0:T(8,128)(2,1)} async-done(((bf16[12,96,96]{2,1,0:T(8,128)(2,1)}), bf16[12,96,96]{2,1,0:T(8,128)(2,1)}, u32[]{:S(2)}, u32[]{:S(2)}) %all-to-all-start) | async-done | bytes 221216 | tf_op jit(solution)/shard_map/all_to_all | solution.py:50
  48.0 1.2 fusion.20
  49.2 1.2 fusion.18
  50.4 0.0 copy-start.2
  50.4 1.2 fusion.17
  51.6 0.0 copy-start.3
  51.6 1.1 fusion.19
  52.8 0.0 copy-done.2
  52.8 0.0 copy-done.3
  52.8 0.0 copy-start.4
  52.8 0.6 copy-done.4
  53.4 4.6 %fusion = bf16[6144,3,96]{0,2,1:T(8,128)(2,1)} fusion(bf16[192,6144]{1,0:T(8,128)(2,1)} %param.5, bf16[1,192,96]{2,1,0:T(8,128)(2,1)S(1)} %fusion.17, bf16[1,192,96]{2,1,0:T(8,128)(2,1)S(1)} %fusion.18, bf16[1,192,96]{2,1,0:T(8,128)(2,1)S(1)} %fusion.19), kind=kOutput, calls=%fused_computation.2 | convolution fusion | flops 681357312 | bytes 6008832 | tf_op jit(solution)/shard_map/tr,pte->rpe/dot_general | solution.py:69
  58.1 0.0 reduce-scatter.2.cloned.1.call-update
  58.1 4.5 %convolution_bitcast_fusion = f32[6144,192]{0,1:T(8,128)} fusion(bf16[6144,3,96]{0,2,1:T(8,128)(2,1)S(1)} %copy-done, bf16[1,192,96]{2,1,0:T(8,128)(2,1)} %copy-done.3, bf16[1,192,96]{2,1,0:T(8,128)(2,1)} %copy-done.2, bf16[1,192,96]{2,1,0:T(8,128)(2,1)} %copy-done.4), kind=kOutput, calls=%fused_computation.1 | convolution fusion | flops 679587840 | bytes 8368128 | tf_op jit(solution)/shard_map/rpe,pte->rt/dot_general | solution.py:72
  62.6 10.8 %reshape.97 = f32[4,8,2,96,192]{3,2,1,0,4:T(2,128)} reshape(f32[6144,192]{0,1:T(8,128)} %convolution_bitcast_fusion) | data formatting | bytes 9437184 | tf_op jit(solution)/shard_map/reshape | solution.py:73
  73.4 7.8 %constant_dynamic-slice_fusion = bf16[4,8,1,96,192]{3,2,1,0,4:T(2,128)(2,1)} fusion(f32[4,8,2,96,192]{3,2,1,0,4:T(2,128)} %reshape.97, s32[]{:T(128)S(6)} %select_n.44), kind=kLoop, calls=%fused_computation.77 | loop fusion | bytes 2359300 | tf_op jit(solution)/shard_map/jit(dynamic_index_in_dim)/dynamic_slice | solution.py:76
  81.3 8.5 %copy.30 = bf16[4,8,1,96,192]{4,3,1,0,2:T(8,128)(2,1)} copy(bf16[4,8,1,96,192]{3,2,1,0,4:T(2,128)(2,1)} %constant_dynamic-slice_fusion) | data formatting | bytes 2359296
  89.8 4.8 %collective-permute-start = (bf16[4,8,96,192]{3,2,1,0:T(8,128)(2,1)}, bf16[4,8,96,192]{3,2,1,0:T(8,128)(2,1)}, u32[]{:S(2)}, u32[]{:S(2)}) collective-permute-start(bf16[4,8,96,192]{3,2,1,0:T(8,128)(2,1)} %bitcast.81), channel_id=1, source_target_pairs={{0,1},{1,0},{2,3},{3,2},{4,5},{5,4},{6,7},{7,6},{8,9},{9,8},{10,11... | collective-permute-start | bytes 3538952 | tf_op jit(solution)/shard_map/ppermute | solution.py:77
  94.6 7.9 %constant_dynamic-slice_fusion.1 = f32[4,8,1,96,192]{3,2,1,0,4:T(1,128)} fusion(f32[4,8,2,96,192]{3,2,1,0,4:T(2,128)} %reshape.97, s32[]{:T(128)S(6)} %select_n.43), kind=kLoop, calls=%fused_computation.78 | loop fusion | bytes 4718596 | tf_op jit(solution)/shard_map/jit(dynamic_index_in_dim)/dynamic_slice | solution.py:75
  102.5 8.9 %copy.21 = f32[4,8,1,96,192]{4,3,1,0,2:T(8,128)} copy(f32[4,8,1,96,192]{3,2,1,0,4:T(1,128)} %constant_dynamic-slice_fusion.1) | data formatting | bytes 4718592 | tf_op jit(solution)/shard_map/jit(dynamic_index_in_dim)/dynamic_slice | solution.py:75
  111.3 0.0 collective-permute-done
  111.3 2.9 %fusion.1 = bf16[4,8,96,192]{3,2,1,0:T(8,128)(2,1)S(1)} fusion(f32[4,8,1,96,192]{4,3,1,0,2:T(8,128)} %copy.21, bf16[4,8,96,192]{3,2,1,0:T(8,128)(2,1)} %collective-permute-done), kind=kLoop, calls=%fused_computation.4 | loop fusion | flops 1769472 | bytes 4718592 | tf_op jit(solution)/shard_map/convert_element_type | solution.py:78
  114.2 24.5 %all_to_all.29 = bf16[4,8,96,192]{3,2,1,0:T(8,128)(2,1)} all-to-all(bf16[4,8,96,192]{3,2,1,0:T(8,128)(2,1)S(1)} %fusion.1), channel_id=1, replica_groups=mesh['seq'=12,'x'=4,'y'=8,'core'=2] {'x'}, dimensions={0} | all-to-all | bytes 2359296 | tf_op jit(solution)/shard_map/all_to_all | solution.py:79
  138.7 2.5 %reduce_sum.111 = bf16[8,96,192]{2,1,0:T(8,128)(2,1)} reduce(bf16[4,8,96,192]{3,2,1,0:T(8,128)(2,1)} %all_to_all.29, bf16[]{:T(256)} %constant.48.clone.1), dimensions={0}, to_apply=%region_7.8 | reduce | flops 442368 | bytes 1474562 | tf_op jit(solution)/shard_map/reduce_sum | solution.py:80
  141.3 20.1 %all_to_all.30 = bf16[8,96,192]{2,1,0:T(8,128)(2,1)} all-to-all(bf16[8,96,192]{2,1,0:T(8,128)(2,1)} %reduce_sum.111), channel_id=1, replica_groups=mesh['seq'=12,'x'=4,'y'=8,'core'=2] {'y'}, dimensions={0} | all-to-all | bytes 589824 | tf_op jit(solution)/shard_map/all_to_all | solution.py:81
  161.4 1.7 reduce_sum.112
  163.1 0.0 reduce-scatter.2.cloned.1.call-done
  163.1 1.7 fusion.22
  164.8 0.7 broadcast_in_dim.100
  165.5 15.1 %all_to_all.31 = f32[64,1,128]{2,1,0:T(1,128)S(1)} all-to-all(f32[64,1,128]{2,1,0:T(1,128)S(1)} %broadcast_in_dim.100), channel_id=1, replica_groups=mesh['seq'=12,'x'=4,'y'=8,'core'=2] {'x','y','core'}, dimensions={0} | all-to-all | bytes 65536 | tf_op jit(solution)/shard_map/all_to_all | solution.py:88
  180.5 0.6 slice_reduce_fusion
  181.1 0.6 broadcast_in_dim.101
  181.8 12.5 %all_to_all.32 = f32[12,8,128]{2,1,0:T(8,128)S(1)} all-to-all(f32[12,8,128]{2,1,0:T(8,128)S(1)} %broadcast_in_dim.101), channel_id=1, replica_groups=mesh['seq'=12,'x'=4,'y'=8,'core'=2] {'seq'}, dimensions={0} | all-to-all | bytes 98304 | tf_op jit(solution)/shard_map/all_to_all | solution.py:90
  194.3 0.6 slice_reduce_fusion.1
  195.6 1.7 fusion.23
  (4 shorter events, 0.0 us)
Async XLA Ops:
  7.2 5.2 %copy-start = (bf16[6144,3,96]{0,2,1:T(8,128)(2,1)S(1)}, bf16[6144,3,96]{0,2,1:T(8,128)(2,1)}, u32[]{:S(2)}) copy-start(bf16[6144,3,96]{0,2,1:T(8,128)(2,1)} %param.6) | copy-start | bytes 10616836
  12.4 3.5 %copy-start.5 = (bf16[192,96]{1,0:T(8,128)(2,1)S(1)}, bf16[192,96]{1,0:T(8,128)(2,1)}, u32[]{:S(2)}) copy-start(bf16[192,96]{1,0:T(8,128)(2,1)} %param.7) | copy-start | bytes 110596
  15.2 0.7 copy-start.1
  17.0 31.0 %all-to-all-start = ((bf16[12,96,96]{2,1,0:T(8,128)(2,1)}), bf16[12,96,96]{2,1,0:T(8,128)(2,1)}, u32[]{:S(2)}, u32[]{:S(2)}) async-start(bf16[12,96,96]{2,1,0:T(8,128)(2,1)} %multiply_convert_fusion), calls=%async_computation | async-start | bytes 589824 | tf_op jit(solution)/shard_map/all_to_all | solution.py:50
  32.7 130.3 %reduce-scatter.2.cloned.1.call-start = ((), (), s32[]{:S(2)}) async-start(), calls=%async_computation.6 | async-start | bytes 3833856 | tf_op jit(solution)/shard_map/reduce_scatter | solution.py:70
  50.4 2.4 %copy-start.2 = (bf16[1,192,96]{2,1,0:T(8,128)(2,1)}, bf16[1,192,96]{2,1,0:T(8,128)(2,1)S(1)}, u32[]{:S(2)}) copy-start(bf16[1,192,96]{2,1,0:T(8,128)(2,1)S(1)} %fusion.18) | copy-start | bytes 110596
  51.6 1.2 copy-start.3
  52.8 0.6 copy-start.4
  89.8 21.5 %collective-permute-start = (bf16[4,8,96,192]{3,2,1,0:T(8,128)(2,1)}, bf16[4,8,96,192]{3,2,1,0:T(8,128)(2,1)}, u32[]{:S(2)}, u32[]{:S(2)}) collective-permute-start(bf16[4,8,96,192]{3,2,1,0:T(8,128)(2,1)} %bitcast.81), channel_id=1, source_target_pairs={{0,1},{1,0},{2,3},{3,2},{4,5},{5,4},{6,7},{7,6},{8,9},{9,8},{10,11... | collective-permute-start | bytes 3538952 | tf_op jit(solution)/shard_map/ppermute | solution.py:77
Sparse Core Ops, SparseCore 0:
  58.2 56.4 reduce-scatter.1

commit v2 on v1

v2 whole, which is shorter than its diff:
```python
import math

import jax
import jax.numpy as jnp
from jax import lax
from jax.experimental import pallas as pl
from jax.experimental.pallas import tpu as pltpu
from jax.sharding import Mesh, PartitionSpec as P

DH = 96
TOK = 192
D = 6144
N_SEQ = 12
NX, NY, NC = 4, 8, 2
N_TENSOR = NX * NY * NC
OUT_ROWS = D // N_TENSOR
HALF = D // NC
PER_X = HALF // NX
PARTS = 3 * DH
K_BLOCK = 1024
S_BLOCK = 1536

DROP_LOGARITHM = 0.3
CLIP_RMS = 0.5
SCALE = DH ** (-0.5)
F32 = jnp.float32
BF16 = jnp.bfloat16
TENSOR = ("x", "y", "core")

NN = (((1,), (0,)), ((), ()))
NT = (((1,), (1,)), ((), ()))
TN = (((0,), (0,)), ((), ()))


def dot(a, b, dims):
    return lax.dot_general(a, b, dims, preferred_element_type=F32)


def split(a):
    high = a.astype(BF16)
    return high, (a - high.astype(F32)).astype(BF16)


def dot_wide_left(a, b, dims):
    high, low = split(a)
    return dot(high, b, dims) + dot(low, b, dims)


def dot_wide_right(a, b, dims):
    high, low = split(b)
    return dot(a, high, dims) + dot(a, low, dims)


def log_decay(rate, events, first, steps):
    seen = jnp.zeros(steps.shape, F32)
    for k in range(events.shape[0]):
        place = events[k] - first
        seen += jnp.where((steps >= place) & (place >= 0), 1.0, 0.0)
    return -(rate * (steps + 1).astype(F32) + DROP_LOGARITHM * seen)


def tail_and_head(rate, events, first):
    steps = lax.broadcasted_iota(jnp.int32, (TOK, 1), 0)
    cumul = log_decay(rate, events, first, steps)
    total = log_decay(rate, events, first, jnp.full((1, 1), TOK - 1, jnp.int32))
    return jnp.exp(total - cumul), jnp.exp(cumul)


def project_kernel(rate_ref, events_ref, x_ref, w_ref, o_ref, qkv_ref, send_ref, acc):
    step = pl.program_id(0)
    term = dot(x_ref[...], w_ref[...], NT)

    @pl.when(step == 0)
    def _():
        acc[...] = term

    @pl.when(step > 0)
    def _():
        acc[...] += term

    @pl.when(step == pl.num_programs(0) - 1)
    def _():
        me = lax.axis_index("seq")
        first = me * TOK
        rate = rate_ref[0]
        proj = acc[...]
        query = (proj[:, :DH] * SCALE).astype(BF16)
        keys = proj[:, DH : 2 * DH].astype(BF16)
        values = proj[:, 2 * DH :].astype(BF16)
        qkv_ref[0] = query
        qkv_ref[1] = keys
        qkv_ref[2] = values
        tail_w, head_w = tail_and_head(rate, events_ref, first)
        forward = dot_wide_left(values.astype(F32) * tail_w, keys, TN)
        reverse = dot_wide_left(query.astype(F32) * head_w, o_ref[...], TN)
        for d in range(N_SEQ):
            low = (jnp.minimum(me, d) + 1) * TOK
            high = jnp.maximum(me, d) * TOK
            count = jnp.float32(0.0)
            for k in range(events_ref.shape[0]):
                inside = (events_ref[k] >= low) & (events_ref[k] < high)
                count += jnp.where(inside, 1.0, 0.0)
            gap = jnp.maximum(high - low, 0).astype(F32)
            weight = jnp.exp(jnp.full((1, DH), -(rate * gap + DROP_LOGARITHM * count), F32))
            send_ref[d] = (jnp.where(d > me, forward, reverse) * weight).astype(BF16)


def local_kernel(rate_ref, events_ref, qkv_ref, o_ref, w_ref, grads_ref, half_ref):
    core = lax.axis_index("core")
    block = w_ref[...]
    for c in range(NC):
        mine = jnp.concatenate(
            [block[:, (y * NC + c) * OUT_ROWS : (y * NC + c + 1) * OUT_ROWS] for y in range(NY)],
            axis=1,
        )
        half_ref[lax.rem(core + c, NC)] = mine

    @pl.when(pl.program_id(0) == 0)
    def _():
        first = lax.axis_index("seq") * TOK
        rate = rate_ref[0]
        row = lax.broadcasted_iota(jnp.int32, (TOK, 1), 0)
        column = lax.broadcasted_iota(jnp.int32, (1, TOK), 1)
        later = row >= column
        gap = log_decay(rate, events_ref, first, row) - log_decay(rate, events_ref, first, column)
        weight = jnp.where(later, jnp.exp(jnp.where(later, gap, 0.0)), 0.0)
        query, keys, values, out = qkv_ref[0], qkv_ref[1], qkv_ref[2], o_ref[...]
        scores = dot(query, keys, NT) * weight
        dscores = dot(out, values, NT) * weight
        grads_ref[0] = dot_wide_left(dscores, keys, NN)
        grads_ref[1] = dot_wide_left(dscores, query, TN)
        grads_ref[2] = dot_wide_left(scores, out, TN)


def weight_kernel(rate_ref, events_ref, got_ref, local_ref, qkv_ref, o_ref, x_ref, grads_ref, terms_ref):
    @pl.when(pl.program_id(0) == 0)
    def _():
        me = lax.axis_index("seq")
        tail_w, head_w = tail_and_head(rate_ref[0], events_ref, me * TOK)
        prefix = jnp.zeros((DH, DH), F32)
        suffix = jnp.zeros((DH, DH), F32)
        for j in range(N_SEQ):
            state = got_ref[j].astype(F32)
            prefix += jnp.where(j < me, state, 0.0)
            suffix += jnp.where(j > me, state, 0.0)
        dquery = local_ref[0] + head_w * dot_wide_right(o_ref[...], prefix, NN)
        dkey = local_ref[1] + tail_w * dot_wide_right(qkv_ref[2], suffix, NT)
        dvalue = local_ref[2] + tail_w * dot_wide_right(qkv_ref[1], suffix, NN)
        grads_ref[...] = jnp.concatenate([dquery * SCALE, dkey, dvalue], axis=1).astype(BF16)

    terms_ref[...] = dot(grads_ref[...], x_ref[...], TN).astype(BF16)


def give_kernel(grads_ref, w_ref, give_ref):
    give_ref[...] = dot(grads_ref[...], w_ref[...], NN).astype(BF16)


def keep_kernel(grads_ref, w_ref, taken_ref, sum_ref):
    sum_ref[...] = (dot(grads_ref[...], w_ref[...], NN) + taken_ref[...].astype(F32)).astype(BF16)


def add_x_kernel(part_ref, out_ref):
    total = part_ref[0].astype(F32)
    for j in range(1, NX):
        total += part_ref[j].astype(F32)
    total = total.T.astype(BF16)
    for y in range(NY):
        out_ref[y] = total[y * OUT_ROWS : (y + 1) * OUT_ROWS]


def add_y_kernel(part_ref, out_ref):
    total = part_ref[0].astype(F32)
    for j in range(1, NY):
        total += part_ref[j].astype(F32)
    out_ref[...] = total.astype(BF16)


SMEM = pl.BlockSpec(memory_space=pltpu.SMEM)


def whole(*shape):
    return pl.BlockSpec(shape, lambda i: (0,) * len(shape))


def shape_of(shape, dtype=BF16):
    return jax.ShapeDtypeStruct(shape, dtype)


def call(kernel, grid, in_specs, out_specs, out_shape, cost, scratch=()):
    flops, moved = cost
    return pl.pallas_call(
        kernel,
        grid=(grid,),
        in_specs=in_specs,
        out_specs=out_specs,
        out_shape=out_shape,
        scratch_shapes=list(scratch),
        compiler_params=pltpu.CompilerParams(
            dimension_semantics=("arbitrary",), vmem_limit_bytes=24 << 20
        ),
        cost_estimate=pl.CostEstimate(flops=flops, bytes_accessed=moved, transcendentals=0),
    )


def project(rate, events, x, w, o):
    return call(
        project_kernel,
        D // K_BLOCK,
        [
            SMEM,
            SMEM,
            pl.BlockSpec((TOK, K_BLOCK), lambda i: (0, i)),
            pl.BlockSpec((PARTS, K_BLOCK), lambda i: (0, i)),
            whole(TOK, DH),
        ],
        [whole(3, TOK, DH), whole(N_SEQ, DH, DH)],
        [shape_of((3, TOK, DH)), shape_of((N_SEQ, DH, DH))],
        (2 * TOK * D * PARTS, 2 * D * (TOK + PARTS)),
        [pltpu.VMEM((TOK, PARTS), F32)],
    )(rate, events, x, w, o)


def local_part(rate, events, qkv, o, w):
    return call(
        local_kernel,
        NX,
        [
            SMEM,
            SMEM,
            whole(3, TOK, DH),
            whole(TOK, DH),
            pl.BlockSpec((PARTS, D // NX), lambda i: (0, i)),
        ],
        [whole(3, TOK, DH), pl.BlockSpec((NC, PARTS, PER_X), lambda i: (0, 0, i))],
        [shape_of((3, TOK, DH), F32), shape_of((NC, PARTS, HALF))],
        (20 * TOK * TOK * DH, 4 * D * PARTS),
    )(rate, events, qkv, o, w)


def weight_terms(rate, events, got, local, qkv, o, x):
    return call(
        weight_kernel,
        D // S_BLOCK,
        [
            SMEM,
            SMEM,
            whole(N_SEQ, DH, DH),
            whole(3, TOK, DH),
            whole(3, TOK, DH),
            whole(TOK, DH),
            pl.BlockSpec((TOK, S_BLOCK), lambda i: (0, i)),
        ],
        [whole(TOK, PARTS), pl.BlockSpec((PARTS, S_BLOCK), lambda i: (0, i))],
        [shape_of((TOK, PARTS)), shape_of((PARTS, D))],
        (2 * TOK * D * PARTS, 2 * D * (TOK + PARTS)),
    )(rate, events, got, local, qkv, o, x)


def half_spec(which):
    return pl.BlockSpec((None, PARTS, PER_X), lambda i: (which, 0, i))


CHUNK = pl.BlockSpec((None, TOK, PER_X), lambda i: (i, 0, 0))


def give_part(grads, halves):
    return call(
        give_kernel,
        NX,
        [whole(TOK, PARTS), half_spec(1)],
        CHUNK,
        shape_of((NX, TOK, PER_X)),
        (TOK * D * PARTS, D * (TOK + PARTS)),
    )(grads, halves)


def keep_part(grads, halves, taken):
    return call(
        keep_kernel,
        NX,
        [whole(TOK, PARTS), half_spec(0), CHUNK],
        CHUNK,
        shape_of((NX, TOK, PER_X)),
        (TOK * D * PARTS, D * (2 * TOK + PARTS)),
    )(grads, halves, taken)


def add_x(parts):
    return call(
        add_x_kernel,
        1,
        [whole(NX, TOK, PER_X)],
        whole(NY, OUT_ROWS, TOK),
        shape_of((NY, OUT_ROWS, TOK)),
        (4 * TOK * PER_X, 10 * TOK * PER_X),
    )(parts)


def add_y(parts):
    return call(
        add_y_kernel,
        1,
        [whole(NY, OUT_ROWS, TOK)],
        whole(OUT_ROWS, TOK),
        shape_of((OUT_ROWS, TOK)),
        (TOK * PER_X, 2 * TOK * PER_X),
    )(parts)


def body(layer_inputs, projection_matrices, result_sensitivity, channel_fading_rate, loss_events):
    x, o, rate, events = layer_inputs, result_sensitivity, channel_fading_rate, loss_events
    w = projection_matrices.transpose(1, 2, 0).reshape(PARTS, D)
    qkv, send = project(rate, events, x, w, o)
    got = lax.all_to_all(send, "seq", 0, 0, tiled=True)
    local, halves = local_part(rate, events, qkv, o, w)
    grads, terms = weight_terms(rate, events, got, local, qkv, o, x)
    summed = lax.psum_scatter(terms, "seq", scatter_dimension=1, tiled=True)

    give = give_part(grads, halves)
    taken = lax.ppermute(give, "core", [(0, 1), (1, 0)])
    part = keep_part(grads, halves, taken)
    part = add_x(lax.all_to_all(part, "x", 0, 0, tiled=True))
    input_grad = add_y(lax.all_to_all(part, "y", 0, 0, tiled=True))

    summed, input_grad = lax.optimization_barrier((summed, input_grad))
    summed = summed.astype(F32)
    square = jnp.sum(summed * summed)
    spread = jnp.broadcast_to(square, (N_TENSOR, 128))
    square = jnp.sum(lax.all_to_all(spread, TENSOR, 0, 0, tiled=True)[:, :1])
    spread = jnp.broadcast_to(square, (N_SEQ, 8, 128))
    square = jnp.sum(lax.all_to_all(spread, "seq", 0, 0, tiled=True)[:, :1, :1])
    factor = jnp.minimum(1.0, CLIP_RMS * math.sqrt(D * PARTS * N_TENSOR) / jnp.sqrt(square + 1e-06))
    weight_grad = (summed * factor).astype(BF16)
    return (input_grad, weight_grad.reshape(3, DH, D // N_SEQ).transpose(2, 0, 1))


def solution(mesh):
    fine = Mesh(mesh.devices.reshape(N_SEQ, NX, NY, NC), ("seq",) + TENSOR)
    return jax.shard_map(
        body,
        mesh=fine,
        in_specs=(P("seq", None), P(None, None, TENSOR), P("seq", TENSOR), P(TENSOR), P()),
        out_specs=(P(TENSOR, "seq"), P("seq", None, TENSOR)),
        check_vma=False,
    )
```

time: 206 us -> 173 us (0.84)
  local copies, waits for them, and re-layouts: 46.4 us -> 21.6 us
  matrix products: 23.5 us -> 0 us
  Pallas kernels: 0 us -> 14.6 us
  other arithmetic: 18.4 us -> 4.66 us
  waiting for transfers between devices: 7.61 us -> 15.6 us
  blocking collectives: 72.1 us -> 79.8 us
    dynamic_slice x3 -> x0, local copies, waits for them, and re-layouts: 24.6 us -> none  [the longest x2 16.7 us: body(): keep = lax.dynamic_index_in_dim(part, core, 2, keepdims=False)]
    dot_general x13 -> x0, matrix products: 23.5 us -> none  [the longest x1 4.64 us: body(): jnp.einsum('tr,pte->rpe', layer_inputs, grads, preferred_element_type=F32)]
    pallas_call x0 -> x7, Pallas kernels: none -> 14.6 us  [the longest x1 4.32 us: project(): call(project_kernel, D // K_BLOCK, [SMEM, SMEM, pl.BlockSpec((TOK, K_BLOC...]
    reshape x1 -> x0, local copies, waits for them, and re-layouts: 10.8 us -> none  [body(): part = part.reshape(NX, NY, NC, width // (NX * NY * NC), row_count)]
    all_to_all x1, blocking collectives: 15.1 us -> 25.9 us  [body(): square = jnp.sum(lax.all_to_all(spread, TENSOR, 0, 0, tiled=True)[:, :1])]
    unnamed x13 -> x42, local copies, waits for them, and re-layouts: 9.66 us -> 20.3 us
    reduce_sum x7 -> x0, other arithmetic: 7.06 us -> none  [the longest x1 2.54 us: body(): part = jnp.sum(part.astype(F32), axis=0).astype(BF16)]
    all_to_all x2, blocking collectives: 44.6 us -> 37.7 us  [the longest x1 19.4 us: body(): part = add_x(lax.all_to_all(part, 'x', 0, 0, tiled=True))]
  transfers between devices with their start and end apart: 3 -> 3, of which waited for: 1 -> 3; matrix products, arithmetic and copies ran while one was open for 31% -> 0% of each run, Pallas kernels for 0% -> 4%
where the time goes in v2:
time: 173 us; the launch traced here: 172 us
  blocking collectives  79.8 us (46%)
  local copies, waits for them, and re-layouts  21.6 us (12%)
  starting transfers between devices  20.4 us (12%)
  waiting for transfers between devices  15.6 us (9%)
  between operations  15.5 us (9%)
  Pallas kernels  14.6 us (8%)
  other arithmetic  4.66 us (3%)
    all_to_all x1, blocking collectives, body(): square = jnp.sum(lax.all_to_all(spread, TENSOR, 0, 0, tiled=True)[:, :1])  25.9 us
    unnamed x42, local copies, waits for them, and re-layouts  20.3 us
    all_to_all x1, blocking collectives, body(): part = add_x(lax.all_to_all(part, 'x', 0, 0, tiled=True))  19.4 us
    all_to_all x1, blocking collectives, body(): input_grad = add_y(lax.all_to_all(part, 'y', 0, 0, tiled=True))  18.3 us
    all_to_all x1, blocking collectives, body(): square = jnp.sum(lax.all_to_all(spread, 'seq', 0, 0, tiled=True)[:, :1, :1])  16.2 us
    all_to_all x1, starting transfers between devices, body(): got = lax.all_to_all(send, 'seq', 0, 0, tiled=True)  15.7 us
    all_to_all x1, waiting for transfers between devices, body(): got = lax.all_to_all(send, 'seq', 0, 0, tiled=True)  7.92 us
    reduce_scatter x1, waiting for transfers between devices, body(): summed = lax.psum_scatter(terms, 'seq', scatter_dimension=1, tiled=True)  5.22 us
  transfers between devices with their start and end apart: 3, of which 3 were waited for; matrix products, arithmetic and copies ran while one was open for 0% of the time, Pallas kernels for 4%

profile of v2, /device:TPU:1, one launch (start us, length us, event | category | flops | bytes accessed | tf_op | source)
XLA Modules:
  0.0 172.2 jit_solution(8310589056936749772)
XLA Ops:
  7.8 0.0 copy-start
  7.8 2.0 %copy-done = bf16[6144,3,96]{0,2,1:T(8,128)(2,1)S(1)} copy-done((bf16[6144,3,96]{0,2,1:T(8,128)(2,1)S(1)}, bf16[6144,3,96]{0,2,1:T(8,128)(2,1)}, u32[]{:S(2)}) %copy-start) | copy-done | bytes 3538968
  9.8 0.0 copy-start.4
  9.8 1.7 copy-done.4
  11.5 0.0 copy-start.13
  11.5 0.8 copy-done.13
  12.3 0.0 copy-start.19
  12.3 0.7 copy-done.19
  12.9 0.0 copy-start.1
  12.9 0.0 copy-start.20
  12.9 4.3 %shard_map.68 = (bf16[3,192,96]{2,1,0:T(8,128)(2,1)S(1)}, bf16[12,96,96]{2,1,0:T(8,128)(2,1)S(1)}) custom-call(f32[1]{0:T(128)S(6)} %copy.11.rate_ref, s32[4]{0:T(128)S(1)} %copy-done.19, bf16[192,6144]{1,0:T(8,128)(2,1)S(1)} %copy-done.4, bf16[288,6144]{1,0:T(8,128)(2,1)S(1)} %bitcast.7, bf16[192,96]{1,0:T(8,128)(2,1)S(1)} %copy-done.13), custom_call_target="tpu_custom_call" | custom-call | flops 679477248 | bytes 5898240 | tf_op jit(solution)/shard_map/pallas_call | solution.py:206
  17.3 0.0 copy-start.10
  17.3 0.6 copy-done.10
  17.9 0.0 copy-start.18
  17.9 0.7 copy-done.18
  18.6 15.7 %all-to-all-start = ((bf16[12,96,96]{2,1,0:T(8,128)(2,1)}), bf16[12,96,96]{2,1,0:T(8,128)(2,1)}, u32[]{:S(2)}, u32[]{:S(2)}) async-start(bf16[12,96,96]{2,1,0:T(8,128)(2,1)} %copy-done.18), calls=%async_computation | async-start | bytes 589824 | tf_op jit(solution)/shard_map/all_to_all | solution.py:314
  34.4 0.0 reduce-scatter.2.cloned.1.call-start
  34.4 0.0 copy-done.1
  34.4 0.0 copy-done.20
  34.4 0.0 copy-start.11
  34.5 0.9 copy-done.11
  35.4 0.0 copy-start.14
  35.4 0.8 copy-done.14
  36.2 3.1 %shard_map.69 = (f32[3,192,96]{2,1,0:T(8,128)S(1)}, bf16[2,288,3072]{2,1,0:T(8,128)(2,1)S(1)}) custom-call(f32[1]{0:T(128)S(6)} %copy.11.rate_ref, s32[4]{0:T(128)S(1)} %copy-done.20, bf16[3,192,96]{2,1,0:T(8,128)(2,1)S(1)} %copy-done.11, bf16[192,96]{1,0:T(8,128)(2,1)S(1)} %copy-done.14, bf16[288,6144]{1,0:T(8,128)(2,1)S(1)} %bitcast.8), custom_call_target="tpu_custom_call" | custom-call | flops 70778880 | bytes 7077888 | tf_op jit(solution)/shard_map/pallas_call | solution.py:224
  39.3 0.0 copy-start.2
  39.3 1.8 %copy-done.2 = bf16[2,288,3072]{2,1,0:T(8,128)(2,1)} copy-done((bf16[2,288,3072]{2,1,0:T(8,128)(2,1)}, bf16[2,288,3072]{2,1,0:T(8,128)(2,1)S(1)}, u32[]{:S(2)}) %copy-start.2) | copy-done | bytes 3538968
  41.0 0.0 copy-start.16
  41.0 0.7 copy-done.16
  41.7 7.9 %all-to-all-done.got_ref = bf16[12,96,96]{2,1,0:T(8,128)(2,1)} async-done(((bf16[12,96,96]{2,1,0:T(8,128)(2,1)}), bf16[12,96,96]{2,1,0:T(8,128)(2,1)}, u32[]{:S(2)}, u32[]{:S(2)}) %all-to-all-start) | async-done | bytes 221216 | tf_op jit(solution)/shard_map/all_to_all | solution.py:314
  49.6 0.0 copy-start.5
  49.7 1.7 copy-done.5
  51.3 0.0 copy-start.12
  51.3 0.9 copy-done.12
  52.2 0.0 copy-start.15
  52.2 0.8 copy-done.15
  53.0 0.0 copy-start.17
  53.0 1.0 copy-done.17
  54.0 3.5 %shard_map.70 = (bf16[192,288]{1,0:T(8,128)(2,1)S(1)}, bf16[288,6144]{1,0:T(8,128)(2,1)S(1)}) custom-call(f32[1]{0:T(128)S(6)} %copy.11.rate_ref, s32[4]{0:T(128)S(1)} %copy-done.20, bf16[12,96,96]{2,1,0:T(8,128)(2,1)} %all-to-all-done.got_ref, f32[3,192,96]{2,1,0:T(8,128)S(1)} %copy-done.17, bf16[3,192,96]{2,1,0:T(8,128)(2,1)S(1)} %copy-done.12, ...), custom_call_target="tpu_custom_call" | custom-call | flops 679477248 | bytes 5898240 | tf_op jit(solution)/shard_map/pallas_call | solution.py:241
  57.5 0.0 copy-start.6
  57.5 1.8 %copy-done.6 = bf16[288,6144]{1,0:T(8,128)(2,1)} copy-done((bf16[288,6144]{1,0:T(8,128)(2,1)}, bf16[288,6144]{1,0:T(8,128)(2,1)S(1)}, u32[]{:S(2)}) %copy-start.6) | copy-done | bytes 3538968
  59.3 0.0 copy-start.7
  59.3 0.7 copy-done.7
  59.9 0.0 copy-start.3
  59.9 0.0 reduce-scatter.2.cloned.1.call-update
  60.0 2.0 %copy-done.3 = bf16[2,288,3072]{2,1,0:T(8,128)(2,1)S(1)} copy-done((bf16[2,288,3072]{2,1,0:T(8,128)(2,1)S(1)}, bf16[2,288,3072]{2,1,0:T(8,128)(2,1)}, u32[]{:S(2)}) %copy-start.3) | copy-done | bytes 3538968
  61.9 0.9 copy-done.8
  62.8 1.4 shard_map.71
  64.3 4.6 %collective-permute-start = (bf16[4,192,768]{2,1,0:T(8,128)(2,1)S(1)}, bf16[4,192,768]{2,1,0:T(8,128)(2,1)S(1)}, u32[]{:S(2)}, u32[]{:S(2)}) collective-permute-start(bf16[4,192,768]{2,1,0:T(8,128)(2,1)S(1)} %shard_map.71), channel_id=1, source_target_pairs={{0,1},{1,0},{2,3},{3,2},{4,5},{5,4},{6,7},{7,6},{8,9},{9,8},{10,11... | collective-permute-start | bytes 3538952 | tf_op jit(solution)/shard_map/ppermute | solution.py:320
  68.9 2.5 %collective-permute-done.taken_ref = bf16[4,192,768]{2,1,0:T(8,128)(2,1)S(1)} collective-permute-done((bf16[4,192,768]{2,1,0:T(8,128)(2,1)S(1)}, bf16[4,192,768]{2,1,0:T(8,128)(2,1)S(1)}, u32[]{:S(2)}, u32[]{:S(2)}) %collective-permute-start) | collective-permute-done | bytes 1179680 | tf_op jit(solution)/shard_map/ppermute | solution.py:320
  71.3 0.0 copy-done.9
  71.3 1.4 shard_map.72
  72.8 19.4 %all_to_all.29.part_ref = bf16[4,192,768]{2,1,0:T(8,128)(2,1)S(1)} all-to-all(bf16[4,192,768]{2,1,0:T(8,128)(2,1)S(1)} %shard_map.72), channel_id=1, replica_groups=mesh['seq'=12,'x'=4,'y'=8,'core'=2] {'x'}, dimensions={0} | all-to-all | bytes 2359296 | tf_op jit(solution)/shard_map/all_to_all | solution.py:322
  92.2 0.2 shard_map.73
  92.4 18.3 %all_to_all.30.part_ref = bf16[8,96,192]{2,1,0:T(8,128)(2,1)S(1)} all-to-all(bf16[8,96,192]{2,1,0:T(8,128)(2,1)S(1)} %shard_map.73), channel_id=1, replica_groups=mesh['seq'=12,'x'=4,'y'=8,'core'=2] {'y'}, dimensions={0} | all-to-all | bytes 589824 | tf_op jit(solution)/shard_map/all_to_all | solution.py:323
  110.7 0.7 shard_map.74
  111.4 5.2 %reduce-scatter.2.cloned.1.call-done = bf16[288,512]{1,0:T(8,128)(2,1)} async-done(((bf16[288,6144]{1,0:T(8,128)(2,1)}), bf16[288,512]{1,0:T(8,128)(2,1)}) %reduce-scatter.2.cloned.1.call-update) | async-done | bytes 294928 | tf_op jit(solution)/shard_map/reduce_scatter | solution.py:317
  116.6 1.7 fusion
  118.3 0.7 broadcast_in_dim.6
  119.0 25.9 %all_to_all.31 = f32[64,1,128]{2,1,0:T(1,128)S(1)} all-to-all(f32[64,1,128]{2,1,0:T(1,128)S(1)} %broadcast_in_dim.6), channel_id=1, replica_groups=mesh['seq'=12,'x'=4,'y'=8,'core'=2] {'x','y','core'}, dimensions={0} | all-to-all | bytes 65536 | tf_op jit(solution)/shard_map/all_to_all | solution.py:329
  144.9 0.6 slice_reduce_fusion
  145.5 0.6 broadcast_in_dim.7
  146.1 16.2 %all_to_all.32 = f32[12,8,128]{2,1,0:T(8,128)S(1)} all-to-all(f32[12,8,128]{2,1,0:T(8,128)S(1)} %broadcast_in_dim.7), channel_id=1, replica_groups=mesh['seq'=12,'x'=4,'y'=8,'core'=2] {'seq'}, dimensions={0} | all-to-all | bytes 98304 | tf_op jit(solution)/shard_map/all_to_all | solution.py:331
  162.3 0.6 slice_reduce_fusion.1
  163.6 1.7 %fusion.1 = bf16[288,512]{1,0:T(8,128)(2,1)} fusion(bf16[288,512]{1,0:T(8,128)(2,1)} %reduce-scatter.2.cloned.1.call-done, f32[]{:T(128)S(6)} %min_shard_map.3), kind=kLoop, calls=%fused_computation.3 | loop fusion | flops 442368 | bytes 589828 | tf_op jit(solution)/shard_map/convert_element_type | solution.py:333
  (2 shorter events, 0.0 us)
Async XLA Ops:
  7.8 2.0 %copy-start = (bf16[6144,3,96]{0,2,1:T(8,128)(2,1)S(1)}, bf16[6144,3,96]{0,2,1:T(8,128)(2,1)}, u32[]{:S(2)}) copy-start(bf16[6144,3,96]{0,2,1:T(8,128)(2,1)} %param.6) | copy-start | bytes 10616836
  9.8 1.7 copy-start.4
  11.5 0.8 copy-start.13
  12.3 0.7 copy-start.19
  12.9 21.5 %copy-start.1 = (bf16[6144,3,96]{0,2,1:T(8,128)(2,1)S(1)}, bf16[6144,3,96]{0,2,1:T(8,128)(2,1)}, u32[]{:S(2)}) copy-start(bf16[6144,3,96]{0,2,1:T(8,128)(2,1)} %param.6) | copy-start | bytes 10616836
  12.9 21.5 %copy-start.20 = (s32[4]{0:T(128)S(1)}, s32[4]{0:T(128)}, u32[]{:S(2)}) copy-start(s32[4]{0:T(128)} %events_ref.5) | copy-start | bytes 52
  17.3 0.7 copy-start.10
  17.9 0.7 copy-start.18
  18.6 31.0 %all-to-all-start = ((bf16[12,96,96]{2,1,0:T(8,128)(2,1)}), bf16[12,96,96]{2,1,0:T(8,128)(2,1)}, u32[]{:S(2)}, u32[]{:S(2)}) async-start(bf16[12,96,96]{2,1,0:T(8,128)(2,1)} %copy-done.18), calls=%async_computation | async-start | bytes 589824 | tf_op jit(solution)/shard_map/all_to_all | solution.py:314
  34.4 82.2 %reduce-scatter.2.cloned.1.call-start = ((), (), s32[]{:S(2)}) async-start(), calls=%async_computation.6 | async-start | bytes 3833856 | tf_op jit(solution)/shard_map/reduce_scatter | solution.py:317
  34.4 0.9 copy-start.11
  35.4 0.8 copy-start.14
  39.3 1.8 %copy-start.2 = (bf16[2,288,3072]{2,1,0:T(8,128)(2,1)}, bf16[2,288,3072]{2,1,0:T(8,128)(2,1)S(1)}, u32[]{:S(2)}) copy-start(bf16[2,288,3072]{2,1,0:T(8,128)(2,1)S(1)} %get-tuple-element.15.w_ref) | copy-start | bytes 10616836
  41.0 0.7 copy-start.16
  49.6 1.7 copy-start.5
  51.3 0.9 copy-start.12
  52.2 0.8 copy-start.15
  53.0 1.0 copy-start.17
  57.5 1.8 %copy-start.6 = (bf16[288,6144]{1,0:T(8,128)(2,1)}, bf16[288,6144]{1,0:T(8,128)(2,1)S(1)}, u32[]{:S(2)}) copy-start(bf16[288,6144]{1,0:T(8,128)(2,1)S(1)} %get-tuple-element.13) | copy-start | bytes 10616836
  59.3 0.7 copy-start.7
  59.9 2.0 %copy-start.3 = (bf16[2,288,3072]{2,1,0:T(8,128)(2,1)S(1)}, bf16[2,288,3072]{2,1,0:T(8,128)(2,1)}, u32[]{:S(2)}) copy-start(bf16[2,288,3072]{2,1,0:T(8,128)(2,1)} %copy-done.2) | copy-start | bytes 10616836
  61.9 0.9 copy-start.8
  62.8 8.5 %copy-start.9 = (bf16[192,288]{1,0:T(8,128)(2,1)S(1)}, bf16[192,288]{1,0:T(8,128)(2,1)}, u32[]{:S(2)}) copy-start(bf16[192,288]{1,0:T(8,128)(2,1)} %copy-done.7) | copy-start | bytes 331780
  64.3 7.1 %collective-permute-start = (bf16[4,192,768]{2,1,0:T(8,128)(2,1)S(1)}, bf16[4,192,768]{2,1,0:T(8,128)(2,1)S(1)}, u32[]{:S(2)}, u32[]{:S(2)}) collective-permute-start(bf16[4,192,768]{2,1,0:T(8,128)(2,1)S(1)} %shard_map.71), channel_id=1, source_target_pairs={{0,1},{1,0},{2,3},{3,2},{4,5},{5,4},{6,7},{7,6},{8,9},{9,8},{10,11... | collective-permute-start | bytes 3538952 | tf_op jit(solution)/shard_map/ppermute | solution.py:320
Sparse Core Ops, SparseCore 0:
  60.1 56.4 reduce-scatter.1

commit v3 on v2

--- a/solution.py
+++ b/solution.py
@@ -19,6 +19,7 @@
 PARTS = 3 * DH
 K_BLOCK = 1024
 S_BLOCK = 1536
+VMEM_LIMIT = 60 << 20
 
 DROP_LOGARITHM = 0.3
 CLIP_RMS = 0.5
@@ -175,6 +176,24 @@
     out_ref[...] = total.astype(BF16)
 
 
+def square_kernel(summed_ref, out_ref):
+    summed = summed_ref[...].astype(F32)
+    total = jnp.sum(jnp.sum(summed * summed, axis=0, keepdims=True), axis=1, keepdims=True)
+    out_ref[...] = jnp.broadcast_to(total, out_ref.shape)
+
+
+def sum_kernel(parts_ref, out_ref):
+    total = jnp.sum(parts_ref[...], axis=0, keepdims=True)
+    out_ref[...] = jnp.broadcast_to(total[None], out_ref.shape)
+
+
+def scale_kernel(parts_ref, summed_ref, out_ref):
+    square = jnp.sum(parts_ref[...], axis=0)[:1, :1]
+    limit = CLIP_RMS * math.sqrt(D * PARTS * N_TENSOR)
+    factor = jnp.minimum(1.0, limit * lax.rsqrt(square + 1e-06))
+    out_ref[...] = (summed_ref[...].astype(F32) * factor).astype(BF16)
+
+
 SMEM = pl.BlockSpec(memory_space=pltpu.SMEM)
 
 
@@ -196,7 +215,7 @@
         out_shape=out_shape,
         scratch_shapes=list(scratch),
         compiler_params=pltpu.CompilerParams(
-            dimension_semantics=("arbitrary",), vmem_limit_bytes=24 << 20
+            dimension_semantics=("arbitrary",), vmem_limit_bytes=VMEM_LIMIT
         ),
         cost_estimate=pl.CostEstimate(flops=flops, bytes_accessed=moved, transcendentals=0),
     )
@@ -307,6 +326,39 @@
     )(parts)
 
 
+def square_of(summed):
+    return call(
+        square_kernel,
+        1,
+        [whole(*summed.shape)],
+        whole(N_TENSOR, 128),
+        shape_of((N_TENSOR, 128), F32),
+        (2 * summed.size, 2 * summed.size),
+    )(summed)
+
+
+def sum_of(parts):
+    return call(
+        sum_kernel,
+        1,
+        [whole(N_TENSOR, 128)],
+        whole(N_SEQ, 8, 128),
+        shape_of((N_SEQ, 8, 128), F32),
+        (N_TENSOR * 128, 4 * N_TENSOR * 128),
+    )(parts)
+
+
+def scaled(parts, summed):
+    return call(
+        scale_kernel,
+        1,
+        [whole(N_SEQ, 8, 128), whole(*summed.shape)],
+        whole(*summed.shape),
+        shape_of(summed.shape),
+        (2 * summed.size, 4 * summed.size),
+    )(parts, summed)
+
+
 def body(layer_inputs, projection_matrices, result_sensitivity, channel_fading_rate, loss_events):
     x, o, rate, events = layer_inputs, result_sensitivity, channel_fading_rate, loss_events
     w = projection_matrices.transpose(1, 2, 0).reshape(PARTS, D)
@@ -323,14 +375,9 @@
     input_grad = add_y(lax.all_to_all(part, "y", 0, 0, tiled=True))
 
     summed, input_grad = lax.optimization_barrier((summed, input_grad))
-    summed = summed.astype(F32)
-    square = jnp.sum(summed * summed)
-    spread = jnp.broadcast_to(square, (N_TENSOR, 128))
-    square = jnp.sum(lax.all_to_all(spread, TENSOR, 0, 0, tiled=True)[:, :1])
-    spread = jnp.broadcast_to(square, (N_SEQ, 8, 128))
-    square = jnp.sum(lax.all_to_all(spread, "seq", 0, 0, tiled=True)[:, :1, :1])
-    factor = jnp.minimum(1.0, CLIP_RMS * math.sqrt(D * PARTS * N_TENSOR) / jnp.sqrt(square + 1e-06))
-    weight_grad = (summed * factor).astype(BF16)
+    square = lax.all_to_all(square_of(summed), TENSOR, 0, 0, tiled=True)
+    square = lax.all_to_all(sum_of(square), "seq", 0, 0, tiled=True)
+    weight_grad = scaled(square, summed)
     return (input_grad, weight_grad.reshape(3, DH, D // N_SEQ).transpose(2, 0, 1))
 
 

time: 173 us -> 164 us (0.948)
  Pallas kernels: 14.6 us -> 35.8 us
  local copies, waits for them, and re-layouts: 21.6 us -> 1.83 us
  other arithmetic: 4.66 us -> 0 us
  waiting for transfers between devices: 15.6 us -> 12 us
    unnamed x42 -> x4, local copies, waits for them, and re-layouts: 20.3 us -> 1.83 us
    reduce_scatter x1, waiting for transfers between devices: 5.22 us -> 0.01 us  [body(): summed = lax.psum_scatter(terms, 'seq', scatter_dimension=1, tiled=True)]
    pallas_call x0 -> x3, Pallas kernels: none -> 4.91 us  [the longest x1 1.83 us: scaled(): call(scale_kernel, 1, [whole(N_SEQ, 8, 128), whole(*summed.shape)], whole...]
    all_to_all x2, blocking collectives: 42.1 us -> 38 us  [the longest x1 21.7 us: body(): square = lax.all_to_all(square_of(summed), TENSOR, 0, 0, tiled=True)]
    pallas_call x1, Pallas kernels: 1.42 us -> 4.37 us  [keep_part(): call(keep_kernel, NX, [whole(TOK, PARTS), half_spec(0), CHUNK], CHUNK, sh...]
    reduce_sum x3 -> x0, other arithmetic: 2.94 us -> none  [the longest x1 1.72 us: body(): square = jnp.sum(summed * summed)]
    pallas_call x1, Pallas kernels: 1.41 us -> 4.19 us  [give_part(): call(give_kernel, NX, [whole(TOK, PARTS), half_spec(1)], CHUNK, shape_of(...]
    pallas_call x1, Pallas kernels: 3.1 us -> 5.83 us  [local_part(): call(local_kernel, NX, [SMEM, SMEM, whole(3, TOK, DH), whole(TOK, DH), pl...]
  transfers between devices with their start and end apart: 3 -> 3, of which waited for: 3 -> 2; matrix products, arithmetic and copies ran while one was open for 0% -> 0% of each run, Pallas kernels for 4% -> 11%
where the time goes in v3:
time: 164 us; the launch traced here: 163 us
  blocking collectives  78.1 us (48%)
  Pallas kernels  35.8 us (22%)
  starting transfers between devices  20.4 us (12%)
  between operations  14.7 us (9%)
  waiting for transfers between devices  12 us (7%)
  local copies, waits for them, and re-layouts  1.83 us (1%)
    all_to_all x1, blocking collectives, body(): square = lax.all_to_all(square_of(summed), TENSOR, 0, 0, tiled=True)  21.7 us
    all_to_all x1, blocking collectives, body(): part = add_x(lax.all_to_all(part, 'x', 0, 0, tiled=True))  20.5 us
    all_to_all x1, blocking collectives, body(): input_grad = add_y(lax.all_to_all(part, 'y', 0, 0, tiled=True))  19.6 us
    all_to_all x1, blocking collectives, body(): square = lax.all_to_all(sum_of(square), 'seq', 0, 0, tiled=True)  16.3 us
    all_to_all x1, starting transfers between devices, body(): got = lax.all_to_all(send, 'seq', 0, 0, tiled=True)  15.7 us
    all_to_all x1, waiting for transfers between devices, body(): got = lax.all_to_all(send, 'seq', 0, 0, tiled=True)  9.28 us
    pallas_call x1, Pallas kernels, project(): call(project_kernel, D // K_BLOCK, [SMEM, SMEM, pl.BlockSpec((TOK, K_BLOC...  6.92 us
    pallas_call x1, Pallas kernels, local_part(): call(local_kernel, NX, [SMEM, SMEM, whole(3, TOK, DH), whole(TOK, DH), pl...  5.83 us
  transfers between devices with their start and end apart: 3, of which 2 were waited for; matrix products, arithmetic and copies ran while one was open for 0% of the time, Pallas kernels for 11%

profile of v3, /device:TPU:1, one launch (start us, length us, event | category | flops | bytes accessed | tf_op | source)
XLA Modules:
  0.0 162.8 jit_solution(14525435975133949585)
XLA Ops:
  7.8 6.9 %shard_map.68 = (bf16[3,192,96]{2,1,0:T(8,128)(2,1)}, bf16[12,96,96]{2,1,0:T(8,128)(2,1)}) custom-call(f32[1]{0:T(128)S(6)} %copy.8.rate_ref, s32[4]{0:T(128)} %events_ref.5, bf16[192,6144]{1,0:T(8,128)(2,1)} %x_ref.3, bf16[288,6144]{1,0:T(8,128)(2,1)} %bitcast.10, bf16[192,96]{1,0:T(8,128)(2,1)} %o_ref.5), custom_call_target="tpu_custom_call" | custom-call | flops 679477248 | bytes 5898240 | tf_op jit(solution)/shard_map/pallas_call | solution.py:225
  14.7 15.7 %all-to-all-start = ((bf16[12,96,96]{2,1,0:T(8,128)(2,1)}), bf16[12,96,96]{2,1,0:T(8,128)(2,1)S(1)}, u32[]{:S(2)}, u32[]{:S(2)}) async-start(bf16[12,96,96]{2,1,0:T(8,128)(2,1)} %get-tuple-element.10), calls=%async_computation | async-start | bytes 589824 | tf_op jit(solution)/shard_map/all_to_all | solution.py:366
  30.4 0.0 reduce-scatter.2.cloned.1.call-start
  30.5 5.8 %shard_map.69 = (f32[3,192,96]{2,1,0:T(8,128)}, bf16[2,288,3072]{2,1,0:T(8,128)(2,1)}) custom-call(f32[1]{0:T(128)S(6)} %copy.8.rate_ref, s32[4]{0:T(128)} %events_ref.5, bf16[3,192,96]{2,1,0:T(8,128)(2,1)} %get-tuple-element.11.qkv_ref, bf16[192,96]{1,0:T(8,128)(2,1)} %o_ref.5, bf16[288,6144]{1,0:T(8,128)(2,1)} %bitcast.11), custom_call_target="tpu_custom_call" | custom-call | flops 70778880 | bytes 7077888 | tf_op jit(solution)/shard_map/pallas_call | solution.py:243
  36.3 9.3 %all-to-all-done.got_ref = bf16[12,96,96]{2,1,0:T(8,128)(2,1)S(1)} async-done(((bf16[12,96,96]{2,1,0:T(8,128)(2,1)}), bf16[12,96,96]{2,1,0:T(8,128)(2,1)S(1)}, u32[]{:S(2)}, u32[]{:S(2)}) %all-to-all-start) | async-done | bytes 221216 | tf_op jit(solution)/shard_map/all_to_all | solution.py:366
  45.6 0.0 copy-start
  45.6 0.7 copy-done
  46.3 5.7 %shard_map.70 = (bf16[192,288]{1,0:T(8,128)(2,1)}, bf16[288,6144]{1,0:T(8,128)(2,1)}) custom-call(f32[1]{0:T(128)S(6)} %copy.8.rate_ref, s32[4]{0:T(128)} %events_ref.5, bf16[12,96,96]{2,1,0:T(8,128)(2,1)} %copy-done, f32[3,192,96]{2,1,0:T(8,128)} %get-tuple-element.12.local_ref, bf16[3,192,96]{2,1,0:T(8,128)(2,1)} %get-tuple-element.11.qkv_ref, ...), custom_call_target="tpu_custom_call" | custom-call | flops 679477248 | bytes 5898240 | tf_op jit(solution)/shard_map/pallas_call | solution.py:260
  52.0 0.0 reduce-scatter.2.cloned.1.call-update
  52.0 4.2 %shard_map.71 = bf16[4,192,768]{2,1,0:T(8,128)(2,1)} custom-call(bf16[192,288]{1,0:T(8,128)(2,1)} %get-tuple-element.14.grads_ref, bf16[2,288,3072]{2,1,0:T(8,128)(2,1)} %get-tuple-element.15.w_ref), custom_call_target="tpu_custom_call" | custom-call | flops 339738624 | bytes 2949120 | tf_op jit(solution)/shard_map/pallas_call | solution.py:286
  56.2 4.6 %collective-permute-start = (bf16[4,192,768]{2,1,0:T(8,128)(2,1)}, bf16[4,192,768]{2,1,0:T(8,128)(2,1)S(1)}, u32[]{:S(2)}, u32[]{:S(2)}) collective-permute-start(bf16[4,192,768]{2,1,0:T(8,128)(2,1)} %shard_map.71), channel_id=1, source_target_pairs={{0,1},{1,0},{2,3},{3,2},{4,5},{5,4},{6,7},{7,6},{8,9},{9,8},{10,11... | collective-permute-start | bytes 3538952 | tf_op jit(solution)/shard_map/ppermute | solution.py:372
  60.8 2.7 %collective-permute-done.taken_ref = bf16[4,192,768]{2,1,0:T(8,128)(2,1)S(1)} collective-permute-done((bf16[4,192,768]{2,1,0:T(8,128)(2,1)}, bf16[4,192,768]{2,1,0:T(8,128)(2,1)S(1)}, u32[]{:S(2)}, u32[]{:S(2)}) %collective-permute-start) | collective-permute-done | bytes 1179680 | tf_op jit(solution)/shard_map/ppermute | solution.py:372
  63.5 0.0 copy-start.1
  63.5 1.1 copy-done.1
  64.6 4.4 %shard_map.72 = bf16[4,192,768]{2,1,0:T(8,128)(2,1)} custom-call(bf16[192,288]{1,0:T(8,128)(2,1)} %get-tuple-element.14.grads_ref, bf16[2,288,3072]{2,1,0:T(8,128)(2,1)} %get-tuple-element.15.w_ref, bf16[4,192,768]{2,1,0:T(8,128)(2,1)} %copy-done.1), custom_call_target="tpu_custom_call" | custom-call | flops 339738624 | bytes 4128768 | tf_op jit(solution)/shard_map/pallas_call | solution.py:297
  69.0 20.5 %all_to_all.31.part_ref = bf16[4,192,768]{2,1,0:T(8,128)(2,1)} all-to-all(bf16[4,192,768]{2,1,0:T(8,128)(2,1)} %shard_map.72), channel_id=1, replica_groups=mesh['seq'=12,'x'=4,'y'=8,'core'=2] {'x'}, dimensions={0} | all-to-all | bytes 2359296 | tf_op jit(solution)/shard_map/all_to_all | solution.py:374
  89.5 2.3 %shard_map.73 = bf16[8,96,192]{2,1,0:T(8,128)(2,1)} custom-call(bf16[4,192,768]{2,1,0:T(8,128)(2,1)} %all_to_all.31.part_ref), custom_call_target="tpu_custom_call" | custom-call | flops 589824 | bytes 1474560 | tf_op jit(solution)/shard_map/pallas_call | solution.py:308
  91.8 19.6 %all_to_all.32.part_ref = bf16[8,96,192]{2,1,0:T(8,128)(2,1)} all-to-all(bf16[8,96,192]{2,1,0:T(8,128)(2,1)} %shard_map.73), channel_id=1, replica_groups=mesh['seq'=12,'x'=4,'y'=8,'core'=2] {'y'}, dimensions={0} | all-to-all | bytes 589824 | tf_op jit(solution)/shard_map/all_to_all | solution.py:375
  111.4 1.7 %shard_map.74 = bf16[96,192]{1,0:T(8,128)(2,1)} custom-call(bf16[8,96,192]{2,1,0:T(8,128)(2,1)} %all_to_all.32.part_ref), custom_call_target="tpu_custom_call" | custom-call | flops 147456 | bytes 294912 | tf_op jit(solution)/shard_map/pallas_call | solution.py:319
  113.0 0.0 reduce-scatter.2.cloned.1.call-done.summed_ref
  113.0 1.7 %shard_map.75 = f32[64,128]{1,0:T(8,128)} custom-call(bf16[288,512]{1,0:T(8,128)(2,1)} %reduce-scatter.2.cloned.1.call-done.summed_ref), custom_call_target="tpu_custom_call" | custom-call | flops 294912 | bytes 294912 | tf_op jit(solution)/shard_map/pallas_call | solution.py:330
  114.7 21.7 %all_to_all.33 = f32[64,1,128]{2,1,0:T(1,128)} all-to-all(f32[64,1,128]{2,1,0:T(1,128)} %bitcast.13), channel_id=1, replica_groups=mesh['seq'=12,'x'=4,'y'=8,'core'=2] {'x','y','core'}, dimensions={0} | all-to-all | bytes 65536 | tf_op jit(solution)/shard_map/all_to_all | solution.py:378
  136.4 1.4 shard_map.76
  137.8 16.3 %all_to_all.34.parts_ref = f32[12,8,128]{2,1,0:T(8,128)} all-to-all(f32[12,8,128]{2,1,0:T(8,128)} %shard_map.76), channel_id=1, replica_groups=mesh['seq'=12,'x'=4,'y'=8,'core'=2] {'seq'}, dimensions={0} | all-to-all | bytes 98304 | tf_op jit(solution)/shard_map/all_to_all | solution.py:379
  154.1 1.8 %shard_map.77 = bf16[288,512]{1,0:T(8,128)(2,1)} custom-call(f32[12,8,128]{2,1,0:T(8,128)} %all_to_all.34.parts_ref, bf16[288,512]{1,0:T(8,128)(2,1)} %reduce-scatter.2.cloned.1.call-done.summed_ref), custom_call_target="tpu_custom_call" | custom-call | flops 294912 | bytes 589824 | tf_op jit(solution)/shard_map/pallas_call | solution.py:352
Async XLA Ops:
  14.7 30.9 %all-to-all-start = ((bf16[12,96,96]{2,1,0:T(8,128)(2,1)}), bf16[12,96,96]{2,1,0:T(8,128)(2,1)S(1)}, u32[]{:S(2)}, u32[]{:S(2)}) async-start(bf16[12,96,96]{2,1,0:T(8,128)(2,1)} %get-tuple-element.10), calls=%async_computation | async-start | bytes 589824 | tf_op jit(solution)/shard_map/all_to_all | solution.py:366
  30.4 82.6 %reduce-scatter.2.cloned.1.call-start = ((), (), s32[]{:S(2)}) async-start(), calls=%async_computation.6 | async-start | bytes 3833856 | tf_op jit(solution)/shard_map/reduce_scatter | solution.py:369
  45.6 0.7 copy-start
  56.2 7.3 %collective-permute-start = (bf16[4,192,768]{2,1,0:T(8,128)(2,1)}, bf16[4,192,768]{2,1,0:T(8,128)(2,1)S(1)}, u32[]{:S(2)}, u32[]{:S(2)}) collective-permute-start(bf16[4,192,768]{2,1,0:T(8,128)(2,1)} %shard_map.71), channel_id=1, source_target_pairs={{0,1},{1,0},{2,3},{3,2},{4,5},{5,4},{6,7},{7,6},{8,9},{9,8},{10,11... | collective-permute-start | bytes 3538952 | tf_op jit(solution)/shard_map/ppermute | solution.py:372
  63.5 1.1 copy-start.1
Sparse Core Ops, SparseCore 0:
  52.1 56.6 reduce-scatter.1

commit v4 on v3

v4 whole, which is shorter than its diff:
```python
import math

import jax
import jax.numpy as jnp
from jax import lax
from jax.experimental import pallas as pl
from jax.experimental.pallas import tpu as pltpu
from jax.sharding import Mesh, PartitionSpec as P

DH = 96
TOK = 192
D = 6144
N_SEQ = 12
NX, NY, NC = 4, 8, 2
N_TENSOR = NX * NY * NC
OUT_ROWS = D // N_TENSOR
HALF = D // NC
PER_X = HALF // NX
PARTS = 3 * DH
K_BLOCK = 1536
S_BLOCK = 1536
PACK_ROWS = 72
PACK_REST = 32
BIG = 60 << 20
MIDDLE = 50 << 20
SMALL = 8 << 20

DROP_LOGARITHM = 0.3
CLIP_RMS = 0.5
SCALE = DH ** (-0.5)
F32 = jnp.float32
BF16 = jnp.bfloat16
TENSOR = ("x", "y", "core")

NN = (((1,), (0,)), ((), ()))
NT = (((1,), (1,)), ((), ()))
TN = (((0,), (0,)), ((), ()))
TT = (((0,), (1,)), ((), ()))


def dot(a, b, dims):
    return lax.dot_general(a, b, dims, preferred_element_type=F32)


def split(a):
    high = a.astype(BF16)
    return high, (a - high.astype(F32)).astype(BF16)


def dot_wide_left(a, b, dims):
    high, low = split(a)
    return dot(high, b, dims) + dot(low, b, dims)


def dot_wide_right(a, b, dims):
    high, low = split(b)
    return dot(a, high, dims) + dot(a, low, dims)


def log_decay(rate, events, first, steps):
    seen = jnp.zeros(steps.shape, F32)
    for k in range(events.shape[0]):
        place = events[k] - first
        seen += jnp.where((steps >= place) & (place >= 0), 1.0, 0.0)
    return -(rate * (steps + 1).astype(F32) + DROP_LOGARITHM * seen)


def tail_and_head(rate, events, first):
    steps = lax.broadcasted_iota(jnp.int32, (1, TOK), 1)
    cumul = log_decay(rate, events, first, steps)
    total = log_decay(rate, events, first, jnp.full((1, 1), TOK - 1, jnp.int32))
    return jnp.exp(total - cumul), jnp.exp(cumul)


def pack(state):
    rest = [state[PACK_ROWS:, k * PACK_REST : (k + 1) * PACK_REST] for k in range(DH // PACK_REST)]
    return jnp.concatenate([state[:PACK_ROWS], jnp.concatenate(rest, axis=0)], axis=1)


def unpack(packed):
    rows = DH - PACK_ROWS
    rest = [packed[k * rows : (k + 1) * rows, DH:] for k in range(DH // PACK_REST)]
    return jnp.concatenate([packed[:, :DH], jnp.concatenate(rest, axis=1)], axis=0)


def columns(k, size):
    return pl.ds(k * size, size)


def fetch(pairs, sems):
    copies = [pltpu.make_async_copy(a, b, sems.at[k]) for k, (a, b) in enumerate(pairs)]
    for copy in copies:
        copy.start()
    return copies


def wait(copies):
    for copy in copies:
        copy.wait()


def project_kernel(
    rate_ref, events_ref, x_ref, w_ref, o_ref, qkv_ref, send_ref,
    x_buf, w_buf, o_buf, acc, sems, o_sem,
):
    copies = []
    for k in range(D // K_BLOCK):
        at = columns(k, K_BLOCK)
        pair = (
            pltpu.make_async_copy(x_ref.at[:, at], x_buf.at[:, at], sems.at[0, k]),
            pltpu.make_async_copy(w_ref.at[:, at], w_buf.at[:, at], sems.at[1, k]),
        )
        for copy in pair:
            copy.start()
        copies.append(pair)
    o_copy = fetch([(o_ref, o_buf)], o_sem)
    for k, pair in enumerate(copies):
        wait(pair)
        at = columns(k, K_BLOCK)
        term = dot(w_buf[:, at], x_buf[:, at], NT)
        if k == 0:
            acc[...] = term
        else:
            acc[...] += term

    me = lax.axis_index("seq")
    rate = rate_ref[0]
    query = (acc[:DH] * SCALE).astype(BF16)
    keys = acc[DH : 2 * DH].astype(BF16)
    values = acc[2 * DH :].astype(BF16)
    qkv_ref[0] = query
    qkv_ref[1] = keys
    qkv_ref[2] = values
    tail_w, head_w = tail_and_head(rate, events_ref, me * TOK)
    forward = pack(dot_wide_left(values.astype(F32) * tail_w, keys, NT))
    wait(o_copy)
    reverse = pack(dot_wide_left(query.astype(F32) * head_w, o_buf[...], NN))
    for d in range(N_SEQ):
        low = (jnp.minimum(me, d) + 1) * TOK
        high = jnp.maximum(me, d) * TOK
        count = jnp.float32(0.0)
        for k in range(events_ref.shape[0]):
            inside = (events_ref[k] >= low) & (events_ref[k] < high)
            count += jnp.where(inside, 1.0, 0.0)
        gap = jnp.maximum(high - low, 0).astype(F32)
        weight = jnp.exp(jnp.full((1, 128), -(rate * gap + DROP_LOGARITHM * count), F32))
        send_ref[d] = (jnp.where(d > me, forward, reverse) * weight).astype(BF16)


def local_kernel(rate_ref, events_ref, qkv_ref, o_ref, w_ref, grads_ref, half_ref):
    core = lax.axis_index("core")
    block = w_ref[...]
    for c in range(NC):
        mine = jnp.concatenate(
            [block[:, (y * NC + c) * OUT_ROWS : (y * NC + c + 1) * OUT_ROWS] for y in range(NY)],
            axis=1,
        )
        half_ref[lax.rem(core + c, NC)] = mine

    @pl.when(pl.program_id(0) == 0)
    def _():
        first = lax.axis_index("seq") * TOK
        rate = rate_ref[0]
        row = lax.broadcasted_iota(jnp.int32, (TOK, 1), 0)
        column = lax.broadcasted_iota(jnp.int32, (1, TOK), 1)
        later = row >= column
        gap = log_decay(rate, events_ref, first, row) - log_decay(rate, events_ref, first, column)
        weight = jnp.where(later, jnp.exp(jnp.where(later, gap, 0.0)), 0.0)
        query, keys, values, out = qkv_ref[0], qkv_ref[1], qkv_ref[2], o_ref[...]
        scores = dot(query, keys, TN) * weight
        dscores = dot(out, values, NN) * weight
        grads_ref[:DH] = dot_wide_right(keys, dscores, NT)
        grads_ref[DH : 2 * DH] = dot_wide_right(query, dscores, NN)
        grads_ref[2 * DH :] = dot_wide_right(out, scores, TN)


def weight_kernel(
    rate_ref, events_ref, got_ref, local_ref, qkv_ref, o_ref, x_ref, grads_ref, terms_ref,
    terms_buf, sems,
):
    me = lax.axis_index("seq")
    tail_w, head_w = tail_and_head(rate_ref[0], events_ref, me * TOK)
    prefix = jnp.zeros((PACK_ROWS, 128), F32)
    suffix = jnp.zeros((PACK_ROWS, 128), F32)
    for j in range(N_SEQ):
        state = got_ref[j].astype(F32)
        prefix += jnp.where(j < me, state, 0.0)
        suffix += jnp.where(j > me, state, 0.0)
    prefix, suffix = unpack(prefix), unpack(suffix)
    dquery = local_ref[:DH] + head_w * dot_wide_left(prefix, o_ref[...], TT)
    dkey = local_ref[DH : 2 * DH] + tail_w * dot_wide_left(suffix, qkv_ref[2], NN)
    dvalue = local_ref[2 * DH :] + tail_w * dot_wide_left(suffix, qkv_ref[1], TN)
    grads_ref[:DH] = (dquery * SCALE).astype(BF16)
    grads_ref[DH : 2 * DH] = dkey.astype(BF16)
    grads_ref[2 * DH :] = dvalue.astype(BF16)

    grads = grads_ref[...]
    sent = []
    for k in range(D // S_BLOCK):
        at = columns(k, S_BLOCK)
        terms_buf[:, at] = dot(grads, x_ref[:, at], NN).astype(BF16)
        copy = pltpu.make_async_copy(terms_buf.at[:, at], terms_ref.at[:, at], sems.at[k])
        copy.start()
        sent.append(copy)
    wait(sent)


def half_copies(w_ref, w_buf, sems, which):
    chunks = [columns(k, PER_X) for k in range(NX)]
    return fetch([(w_ref.at[which, :, at], w_buf.at[:, at]) for at in chunks], sems)


def give_kernel(grads_ref, w_ref, give_ref, w_buf, sems):
    grads = grads_ref[...]
    for k, copy in enumerate(half_copies(w_ref, w_buf, sems, 1)):
        wait([copy])
        give_ref[k] = dot(grads, w_buf[:, columns(k, PER_X)], TN).astype(BF16)


def keep_kernel(grads_ref, w_ref, taken_ref, sum_ref, w_buf, sems):
    grads = grads_ref[...]
    for k, copy in enumerate(half_copies(w_ref, w_buf, sems, 0)):
        wait([copy])
        mine = dot(grads, w_buf[:, columns(k, PER_X)], TN)
        sum_ref[k] = (mine + taken_ref[k].astype(F32)).astype(BF16)


def add_x_kernel(part_ref, out_ref):
    total = part_ref[0].astype(F32)
    for j in range(1, NX):
        total += part_ref[j].astype(F32)
    total = total.T.astype(BF16)
    for y in range(NY):
        out_ref[y] = total[y * OUT_ROWS : (y + 1) * OUT_ROWS]


def add_y_kernel(part_ref, out_ref):
    total = part_ref[0].astype(F32)
    for j in range(1, NY):
        total += part_ref[j].astype(F32)
    out_ref[...] = total.astype(BF16)


def square_kernel(summed_ref, out_ref, held_ref):
    held_ref[...] = summed_ref[...]
    summed = summed_ref[...].astype(F32)
    total = jnp.sum(jnp.sum(summed * summed, axis=0, keepdims=True), axis=1, keepdims=True)
    out_ref[...] = jnp.broadcast_to(total, out_ref.shape)


def sum_kernel(parts_ref, out_ref):
    total = jnp.sum(parts_ref[...], axis=0, keepdims=True)
    for j in range(N_SEQ):
        out_ref[j] = total


def scale_kernel(parts_ref, summed_ref, out_ref):
    square = parts_ref[0]
    for j in range(1, N_SEQ):
        square += parts_ref[j]
    square = square[:, :1]
    limit = CLIP_RMS * math.sqrt(D * PARTS * N_TENSOR)
    factor = jnp.minimum(1.0, limit * lax.rsqrt(square + 1e-06))
    out_ref[...] = (summed_ref[...].astype(F32) * factor).astype(BF16)


SMEM = pl.BlockSpec(memory_space=pltpu.SMEM)
VMEM = pl.BlockSpec(memory_space=pltpu.VMEM)
HBM = pl.BlockSpec(memory_space=pltpu.HBM)
DMA = pltpu.SemaphoreType.DMA


def shape_of(shape, dtype=BF16):
    return jax.ShapeDtypeStruct(shape, dtype)


def call(kernel, in_specs, out_specs, out_shape, cost, scratch=(), limit=BIG, **grid):
    flops, moved = cost
    return pl.pallas_call(
        kernel,
        in_specs=in_specs,
        out_specs=out_specs,
        out_shape=out_shape,
        scratch_shapes=list(scratch),
        compiler_params=pltpu.CompilerParams(vmem_limit_bytes=limit),
        cost_estimate=pl.CostEstimate(flops=flops, bytes_accessed=moved, transcendentals=0),
        **grid,
    )


def project(rate, events, x, w, o):
    return call(
        project_kernel,
        [SMEM, SMEM, HBM, HBM, HBM],
        [VMEM, VMEM],
        [shape_of((3, DH, TOK)), shape_of((N_SEQ, PACK_ROWS, 128))],
        (2 * TOK * D * PARTS, 2 * D * (TOK + PARTS)),
        [
            pltpu.VMEM((TOK, D), BF16),
            pltpu.VMEM((PARTS, D), BF16),
            pltpu.VMEM((TOK, DH), BF16),
            pltpu.VMEM((PARTS, TOK), F32),
            DMA((2, D // K_BLOCK)),
            DMA((1,)),
        ],
    )(rate, events, x, w, o)


def local_part(rate, events, qkv, o, w):
    def whole(*shape):
        return pl.BlockSpec(shape, lambda i: (0,) * len(shape))

    return call(
        local_kernel,
        [
            SMEM,
            SMEM,
            whole(3, DH, TOK),
            whole(TOK, DH),
            pl.BlockSpec((PARTS, D // NX), lambda i: (0, i)),
        ],
        [whole(PARTS, TOK), pl.BlockSpec((NC, PARTS, PER_X), lambda i: (0, 0, i))],
        [shape_of((PARTS, TOK), F32), shape_of((NC, PARTS, HALF))],
        (20 * TOK * TOK * DH, 4 * D * PARTS),
        grid=(NX,),
    )(rate, events, qkv, o, w)


def weight_terms(rate, events, got, local, qkv, o, x):
    return call(
        weight_kernel,
        [SMEM, SMEM, VMEM, VMEM, VMEM, VMEM, VMEM],
        [VMEM, HBM],
        [shape_of((PARTS, TOK)), shape_of((PARTS, D))],
        (2 * TOK * D * PARTS, 2 * D * (TOK + PARTS)),
        [
            pltpu.VMEM((PARTS, D), BF16),
            DMA((D // S_BLOCK,)),
        ],
        limit=MIDDLE,
    )(rate, events, got, local, qkv, o, x)


def give_part(grads, halves):
    return call(
        give_kernel,
        [VMEM, HBM],
        VMEM,
        shape_of((NX, TOK, PER_X)),
        (TOK * D * PARTS, D * (TOK + PARTS)),
        [pltpu.VMEM((PARTS, HALF), BF16), DMA((NX,))],
        limit=MIDDLE,
    )(grads, halves)


def keep_part(grads, halves, taken):
    return call(
        keep_kernel,
        [VMEM, HBM, VMEM],
        VMEM,
        shape_of((NX, TOK, PER_X)),
        (TOK * D * PARTS, D * (2 * TOK + PARTS)),
        [pltpu.VMEM((PARTS, HALF), BF16), DMA((NX,))],
        limit=MIDDLE,
    )(grads, halves, taken)


def add_x(parts):
    shape = (NY, OUT_ROWS, TOK)
    return call(
        add_x_kernel, [VMEM], VMEM, shape_of(shape), (4 * parts.size, 4 * parts.size), limit=SMALL
    )(parts)


def add_y(parts):
    shape = (OUT_ROWS, TOK)
    return call(
        add_y_kernel, [VMEM], VMEM, shape_of(shape), (parts.size, 2 * parts.size), limit=SMALL
    )(parts)


def square_of(summed):
    return call(
        square_kernel,
        [VMEM],
        [VMEM, VMEM],
        [shape_of((N_TENSOR, 128), F32), shape_of(summed.shape)],
        (2 * summed.size, 2 * summed.size),
        limit=SMALL,
    )(summed)


def sum_of(parts):
    return call(
        sum_kernel, [VMEM], VMEM, shape_of((N_SEQ, 1, 128), F32), (parts.size, 4 * parts.size), limit=SMALL
    )(parts)


def scaled(parts, summed):
    return call(
        scale_kernel,
        [VMEM, VMEM],
        VMEM,
        shape_of(summed.shape),
        (2 * summed.size, 4 * summed.size),
        limit=SMALL,
    )(parts, summed)


def body(layer_inputs, projection_matrices, result_sensitivity, channel_fading_rate, loss_events):
    x, o, rate, events = layer_inputs, result_sensitivity, channel_fading_rate, loss_events
    w = projection_matrices.transpose(1, 2, 0).reshape(PARTS, D)
    qkv, send = project(rate, events, x, w, o)
    got = lax.all_to_all(send, "seq", 0, 0, tiled=True)
    local, halves = local_part(rate, events, qkv, o, w)
    grads, terms = weight_terms(rate, events, got, local, qkv, o, x)
    summed = lax.psum_scatter(terms, "seq", scatter_dimension=1, tiled=True)

    give = give_part(grads, halves)
    taken = lax.ppermute(give, "core", [(0, 1), (1, 0)])
    part = keep_part(grads, halves, taken)
    part = add_x(lax.all_to_all(part, "x", 0, 0, tiled=True))
    input_grad = add_y(lax.all_to_all(part, "y", 0, 0, tiled=True))

    summed, input_grad = lax.optimization_barrier((summed, input_grad))
    square, summed = square_of(summed)
    square = lax.all_to_all(square, TENSOR, 0, 0, tiled=True)
    square = lax.all_to_all(sum_of(square), "seq", 0, 0, tiled=True)
    weight_grad = scaled(square, summed)
    return (input_grad, weight_grad.reshape(3, DH, D // N_SEQ).transpose(2, 0, 1))


def solution(mesh):
    fine = Mesh(mesh.devices.reshape(N_SEQ, NX, NY, NC), ("seq",) + TENSOR)
    return jax.shard_map(
        body,
        mesh=fine,
        in_specs=(P("seq", None), P(None, None, TENSOR), P("seq", TENSOR), P(TENSOR), P()),
        out_specs=(P(TENSOR, "seq"), P("seq", None, TENSOR)),
        check_vma=False,
    )
```

time: 164 us -> 154 us (0.939)
  Pallas kernels: 35.8 us -> 21.9 us
  waiting for transfers between devices: 12 us -> 15.5 us
    pallas_call x10, Pallas kernels: 35.8 us -> 21.9 us  [the longest x1 5.96 us: project(): call(project_kernel, [SMEM, SMEM, HBM, HBM, HBM], [VMEM, VMEM], [shape_of...]
    reduce_scatter x1, waiting for transfers between devices: 0.01 us -> 6.03 us  [body(): summed = lax.psum_scatter(terms, 'seq', scatter_dimension=1, tiled=True)]
    all_to_all x1, blocking collectives: 21.7 us -> 25.9 us  [body(): square = lax.all_to_all(square, TENSOR, 0, 0, tiled=True)]
    all_to_all x1, waiting for transfers between devices: 9.28 us -> 7.04 us  [body(): got = lax.all_to_all(send, 'seq', 0, 0, tiled=True)]
  transfers between devices with their start and end apart: 3 -> 3, of which waited for: 2 -> 3; matrix products, arithmetic and copies ran while one was open for 0% -> 0% of each run, Pallas kernels for 11% -> 8%
where the time goes in v4:
time: 154 us; the launch traced here: 153 us
  blocking collectives  78.7 us (51%)
  Pallas kernels  21.9 us (14%)
  starting transfers between devices  20.6 us (13%)
  waiting for transfers between devices  15.5 us (10%)
  between operations  14.8 us (10%)
  local copies, waits for them, and re-layouts  1.94 us (1%)
    all_to_all x1, blocking collectives, body(): square = lax.all_to_all(square, TENSOR, 0, 0, tiled=True)  25.9 us
    all_to_all x1, blocking collectives, body(): part = add_x(lax.all_to_all(part, 'x', 0, 0, tiled=True))  19.5 us
    all_to_all x1, blocking collectives, body(): input_grad = add_y(lax.all_to_all(part, 'y', 0, 0, tiled=True))  18.2 us
    all_to_all x1, starting transfers between devices, body(): got = lax.all_to_all(send, 'seq', 0, 0, tiled=True)  15.8 us
    all_to_all x1, blocking collectives, body(): square = lax.all_to_all(sum_of(square), 'seq', 0, 0, tiled=True)  15.1 us
    all_to_all x1, waiting for transfers between devices, body(): got = lax.all_to_all(send, 'seq', 0, 0, tiled=True)  7.04 us
    reduce_scatter x1, waiting for transfers between devices, body(): summed = lax.psum_scatter(terms, 'seq', scatter_dimension=1, tiled=True)  6.03 us
    pallas_call x1, Pallas kernels, project(): call(project_kernel, [SMEM, SMEM, HBM, HBM, HBM], [VMEM, VMEM], [shape_of...  5.96 us
  transfers between devices with their start and end apart: 3, of which 3 were waited for; matrix products, arithmetic and copies ran while one was open for 0% of the time, Pallas kernels for 8%

profile of v4, /device:TPU:1, one launch (start us, length us, event | category | flops | bytes accessed | tf_op | source)
XLA Modules:
  0.0 153.4 jit_solution(2068703596470964264)
XLA Ops:
  7.8 6.0 %shard_map.68 = (bf16[3,96,192]{2,1,0:T(8,128)(2,1)}, bf16[12,72,128]{2,1,0:T(8,128)(2,1)}) custom-call(f32[1]{0:T(128)S(6)} %copy.8.rate_ref, s32[4]{0:T(128)} %events_ref.5, bf16[192,6144]{1,0:T(8,128)(2,1)} %x_ref.3, bf16[288,6144]{1,0:T(8,128)(2,1)} %bitcast.12, bf16[192,96]{1,0:T(8,128)(2,1)} %o_ref.5), custom_call_target="tpu_custom_call" | custom-call | flops 679477248 | bytes 5898240 | tf_op jit(solution)/shard_map/pallas_call | solution.py:292
  13.8 0.0 copy-start
  13.8 0.0 copy-start.1
  13.8 0.0 copy-start.2
  13.8 0.0 copy-start.5
  13.8 15.8 %all-to-all-start = ((bf16[12,72,128]{2,1,0:T(8,128)(2,1)}), bf16[12,72,128]{2,1,0:T(8,128)(2,1)S(1)}, u32[]{:S(2)}, u32[]{:S(2)}) async-start(bf16[12,72,128]{2,1,0:T(8,128)(2,1)} %get-tuple-element.12), calls=%async_computation | async-start | bytes 442368 | tf_op jit(solution)/shard_map/all_to_all | solution.py:414
  29.7 0.0 reduce-scatter.2.cloned.1.call-start
  29.7 5.7 %shard_map.69 = (f32[288,192]{1,0:T(8,128)}, bf16[2,288,3072]{2,1,0:T(8,128)(2,1)}) custom-call(f32[1]{0:T(128)S(6)} %copy.8.rate_ref, s32[4]{0:T(128)} %events_ref.5, bf16[3,96,192]{2,1,0:T(8,128)(2,1)} %get-tuple-element.13.qkv_ref, bf16[192,96]{1,0:T(8,128)(2,1)} %o_ref.5, bf16[288,6144]{1,0:T(8,128)(2,1)} %bitcast.13), custom_call_target="tpu_custom_call" | custom-call | flops 70778880 | bytes 7077888 | tf_op jit(solution)/shard_map/pallas_call | solution.py:313
  35.5 7.0 %all-to-all-done.got_ref = bf16[12,72,128]{2,1,0:T(8,128)(2,1)S(1)} async-done(((bf16[12,72,128]{2,1,0:T(8,128)(2,1)}), bf16[12,72,128]{2,1,0:T(8,128)(2,1)S(1)}, u32[]{:S(2)}, u32[]{:S(2)}) %all-to-all-start) | async-done | bytes 221216 | tf_op jit(solution)/shard_map/all_to_all | solution.py:414
  42.5 0.0 copy-done
  42.5 0.0 copy-done.1
  42.5 0.0 copy-done.2
  42.5 0.0 copy-done.5
  42.5 0.0 copy-start.4
  42.5 1.0 copy-done.4
  43.5 3.1 %shard_map.70 = (bf16[288,192]{1,0:T(8,128)(2,1)S(1)}, bf16[288,6144]{1,0:T(8,128)(2,1)}) custom-call(f32[1]{0:T(128)S(6)} %copy.8.rate_ref, s32[4]{0:T(128)S(1)} %copy-done.5, bf16[12,72,128]{2,1,0:T(8,128)(2,1)S(1)} %all-to-all-done.got_ref, f32[288,192]{1,0:T(8,128)S(1)} %copy-done.4, bf16[3,96,192]{2,1,0:T(8,128)(2,1)S(1)} %copy-done.1, ...), custom_call_target="tpu_custom_call" | custom-call | flops 679477248 | bytes 5898240 | tf_op jit(solution)/shard_map/pallas_call | solution.py:330
  46.6 0.0 reduce-scatter.2.cloned.1.call-update
  46.7 2.6 %shard_map.71 = bf16[4,192,768]{2,1,0:T(8,128)(2,1)S(1)} custom-call(bf16[288,192]{1,0:T(8,128)(2,1)S(1)} %get-tuple-element.16.grads_ref, bf16[2,288,3072]{2,1,0:T(8,128)(2,1)} %get-tuple-element.17.w_ref), custom_call_target="tpu_custom_call" | custom-call | flops 339738624 | bytes 2949120 | tf_op jit(solution)/shard_map/pallas_call | solution.py:345
  49.2 4.7 %collective-permute-start = (bf16[4,192,768]{2,1,0:T(8,128)(2,1)S(1)}, bf16[4,192,768]{2,1,0:T(8,128)(2,1)S(1)}, u32[]{:S(2)}, u32[]{:S(2)}) collective-permute-start(bf16[4,192,768]{2,1,0:T(8,128)(2,1)S(1)} %shard_map.71), channel_id=1, source_target_pairs={{0,1},{1,0},{2,3},{3,2},{4,5},{5,4},{6,7},{7,6},{8,9},{9,8},{10,11... | collective-permute-start | bytes 3538952 | tf_op jit(solution)/shard_map/ppermute | solution.py:420
  53.9 2.5 %collective-permute-done.taken_ref = bf16[4,192,768]{2,1,0:T(8,128)(2,1)S(1)} collective-permute-done((bf16[4,192,768]{2,1,0:T(8,128)(2,1)S(1)}, bf16[4,192,768]{2,1,0:T(8,128)(2,1)S(1)}, u32[]{:S(2)}, u32[]{:S(2)}) %collective-permute-start) | collective-permute-done | bytes 1179680 | tf_op jit(solution)/shard_map/ppermute | solution.py:420
  56.4 2.6 %shard_map.72 = bf16[4,192,768]{2,1,0:T(8,128)(2,1)S(1)} custom-call(bf16[288,192]{1,0:T(8,128)(2,1)S(1)} %get-tuple-element.16.grads_ref, bf16[2,288,3072]{2,1,0:T(8,128)(2,1)} %get-tuple-element.17.w_ref, bf16[4,192,768]{2,1,0:T(8,128)(2,1)S(1)} %collective-permute-done.taken_ref), custom_call_target="tpu_custom_call" | custom-call | flops 339738624 | bytes 4128768 | tf_op jit(solution)/shard_map/pallas_call | solution.py:357
  59.0 19.5 %all_to_all.31.part_ref = bf16[4,192,768]{2,1,0:T(8,128)(2,1)S(1)} all-to-all(bf16[4,192,768]{2,1,0:T(8,128)(2,1)S(1)} %shard_map.72), channel_id=1, replica_groups=mesh['seq'=12,'x'=4,'y'=8,'core'=2] {'x'}, dimensions={0} | all-to-all | bytes 2359296 | tf_op jit(solution)/shard_map/all_to_all | solution.py:422
  78.4 0.2 shard_map.73
  78.7 18.2 %all_to_all.32.part_ref = bf16[8,96,192]{2,1,0:T(8,128)(2,1)S(1)} all-to-all(bf16[8,96,192]{2,1,0:T(8,128)(2,1)S(1)} %shard_map.73), channel_id=1, replica_groups=mesh['seq'=12,'x'=4,'y'=8,'core'=2] {'y'}, dimensions={0} | all-to-all | bytes 589824 | tf_op jit(solution)/shard_map/all_to_all | solution.py:423
  96.9 0.7 shard_map.74
  97.6 6.0 %reduce-scatter.2.cloned.1.call-done.summed_ref = bf16[288,512]{1,0:T(8,128)(2,1)} async-done(((bf16[288,6144]{1,0:T(8,128)(2,1)}), bf16[288,512]{1,0:T(8,128)(2,1)}) %reduce-scatter.2.cloned.1.call-update) | async-done | bytes 294928 | tf_op jit(solution)/shard_map/reduce_scatter | solution.py:417
  103.6 0.0 copy-start.3
  103.6 1.0 copy-done.3
  104.6 0.1 shard_map.75
  104.7 25.9 %all_to_all.33 = f32[64,1,128]{2,1,0:T(1,128)S(1)} all-to-all(f32[64,1,128]{2,1,0:T(1,128)S(1)} %bitcast.11), channel_id=1, replica_groups=mesh['seq'=12,'x'=4,'y'=8,'core'=2] {'x','y','core'}, dimensions={0} | all-to-all | bytes 65536 | tf_op jit(solution)/shard_map/all_to_all | solution.py:427
  130.6 15.1 %all_to_all.34.parts_ref = f32[12,1,128]{2,1,0:T(1,128)S(1)} all-to-all(f32[12,1,128]{2,1,0:T(1,128)S(1)} %shard_map.76), channel_id=1, replica_groups=mesh['seq'=12,'x'=4,'y'=8,'core'=2] {'seq'}, dimensions={0} | all-to-all | bytes 12288 | tf_op jit(solution)/shard_map/all_to_all | solution.py:428
  145.7 0.9 shard_map.77
  (1 shorter events, 0.0 us)
Async XLA Ops:
  13.8 28.7 %copy-start = (bf16[192,6144]{1,0:T(8,128)(2,1)S(1)}, bf16[192,6144]{1,0:T(8,128)(2,1)}, u32[]{:S(2)}) copy-start(bf16[192,6144]{1,0:T(8,128)(2,1)} %x_ref.3) | copy-start | bytes 7077892
  13.8 28.7 %copy-start.1 = (bf16[3,96,192]{2,1,0:T(8,128)(2,1)S(1)}, bf16[3,96,192]{2,1,0:T(8,128)(2,1)}, u32[]{:S(2)}) copy-start(bf16[3,96,192]{2,1,0:T(8,128)(2,1)} %get-tuple-element.13.qkv_ref) | copy-start | bytes 331780
  13.8 28.7 %copy-start.2 = (bf16[192,96]{1,0:T(8,128)(2,1)S(1)}, bf16[192,96]{1,0:T(8,128)(2,1)}, u32[]{:S(2)}) copy-start(bf16[192,96]{1,0:T(8,128)(2,1)} %o_ref.5) | copy-start | bytes 110596
  13.8 28.7 %copy-start.5 = (s32[4]{0:T(128)S(1)}, s32[4]{0:T(128)}, u32[]{:S(2)}) copy-start(s32[4]{0:T(128)} %events_ref.5) | copy-start | bytes 52
  13.8 28.7 %all-to-all-start = ((bf16[12,72,128]{2,1,0:T(8,128)(2,1)}), bf16[12,72,128]{2,1,0:T(8,128)(2,1)S(1)}, u32[]{:S(2)}, u32[]{:S(2)}) async-start(bf16[12,72,128]{2,1,0:T(8,128)(2,1)} %get-tuple-element.12), calls=%async_computation | async-start | bytes 442368 | tf_op jit(solution)/shard_map/all_to_all | solution.py:414
  29.7 73.9 %reduce-scatter.2.cloned.1.call-start = ((), (), s32[]{:S(2)}) async-start(), calls=%async_computation.6 | async-start | bytes 3833856 | tf_op jit(solution)/shard_map/reduce_scatter | solution.py:417
  42.5 1.0 copy-start.4
  49.2 7.2 %collective-permute-start = (bf16[4,192,768]{2,1,0:T(8,128)(2,1)S(1)}, bf16[4,192,768]{2,1,0:T(8,128)(2,1)S(1)}, u32[]{:S(2)}, u32[]{:S(2)}) collective-permute-start(bf16[4,192,768]{2,1,0:T(8,128)(2,1)S(1)} %shard_map.71), channel_id=1, source_target_pairs={{0,1},{1,0},{2,3},{3,2},{4,5},{5,4},{6,7},{7,6},{8,9},{9,8},{10,11... | collective-permute-start | bytes 3538952 | tf_op jit(solution)/shard_map/ppermute | solution.py:420
  103.6 1.0 copy-start.3
Sparse Core Ops, SparseCore 0:
  46.8 56.7 reduce-scatter.1

commit v5 on v4

--- a/solution.py
+++ b/solution.py
@@ -245,20 +245,19 @@
     held_ref[...] = summed_ref[...]
     summed = summed_ref[...].astype(F32)
     total = jnp.sum(jnp.sum(summed * summed, axis=0, keepdims=True), axis=1, keepdims=True)
+    for j in range(N_SEQ):
+        out_ref[j] = jnp.broadcast_to(total, (1, 128))
+
+
+def sum_kernel(parts_ref, out_ref):
+    total = parts_ref[0]
+    for j in range(1, N_SEQ):
+        total += parts_ref[j]
     out_ref[...] = jnp.broadcast_to(total, out_ref.shape)
 
 
-def sum_kernel(parts_ref, out_ref):
-    total = jnp.sum(parts_ref[...], axis=0, keepdims=True)
-    for j in range(N_SEQ):
-        out_ref[j] = total
-
-
 def scale_kernel(parts_ref, summed_ref, out_ref):
-    square = parts_ref[0]
-    for j in range(1, N_SEQ):
-        square += parts_ref[j]
-    square = square[:, :1]
+    square = jnp.sum(parts_ref[...], axis=0, keepdims=True)[:, :1]
     limit = CLIP_RMS * math.sqrt(D * PARTS * N_TENSOR)
     factor = jnp.minimum(1.0, limit * lax.rsqrt(square + 1e-06))
     out_ref[...] = (summed_ref[...].astype(F32) * factor).astype(BF16)
@@ -322,6 +321,7 @@
         [whole(PARTS, TOK), pl.BlockSpec((NC, PARTS, PER_X), lambda i: (0, 0, i))],
         [shape_of((PARTS, TOK), F32), shape_of((NC, PARTS, HALF))],
         (20 * TOK * TOK * DH, 4 * D * PARTS),
+        limit=MIDDLE,
         grid=(NX,),
     )(rate, events, qkv, o, w)
 
@@ -384,7 +384,7 @@
         square_kernel,
         [VMEM],
         [VMEM, VMEM],
-        [shape_of((N_TENSOR, 128), F32), shape_of(summed.shape)],
+        [shape_of((N_SEQ, 1, 128), F32), shape_of(summed.shape)],
         (2 * summed.size, 2 * summed.size),
         limit=SMALL,
     )(summed)
@@ -392,7 +392,7 @@
 
 def sum_of(parts):
     return call(
-        sum_kernel, [VMEM], VMEM, shape_of((N_SEQ, 1, 128), F32), (parts.size, 4 * parts.size), limit=SMALL
+        sum_kernel, [VMEM], VMEM, shape_of((N_TENSOR, 128), F32), (parts.size, 4 * parts.size), limit=SMALL
     )(parts)
 
 
@@ -424,8 +424,8 @@
 
     summed, input_grad = lax.optimization_barrier((summed, input_grad))
     square, summed = square_of(summed)
-    square = lax.all_to_all(square, TENSOR, 0, 0, tiled=True)
-    square = lax.all_to_all(sum_of(square), "seq", 0, 0, tiled=True)
+    square = lax.all_to_all(square, "seq", 0, 0, tiled=True)
+    square = lax.all_to_all(sum_of(square), TENSOR, 0, 0, tiled=True)
     weight_grad = scaled(square, summed)
     return (input_grad, weight_grad.reshape(3, DH, D // N_SEQ).transpose(2, 0, 1))
 

time: 154 us -> 155 us (level)
  local copies, waits for them, and re-layouts: 1.94 us -> 3.62 us
    unnamed x12 -> x14, local copies, waits for them, and re-layouts: 1.94 us -> 3.62 us
  transfers between devices with their start and end apart: 3 -> 3, of which waited for: 3 -> 3; matrix products, arithmetic and copies ran while one was open for 0% -> 0% of each run, Pallas kernels for 8% -> 7%
where the time goes in v5:
time: 155 us; the launch traced here: 154 us
  blocking collectives  80.2 us (52%)
  starting transfers between devices  20.6 us (13%)
  Pallas kernels  20.4 us (13%)
  between operations  14.8 us (10%)
  waiting for transfers between devices  14.4 us (9%)
  local copies, waits for them, and re-layouts  3.62 us (2%)
    all_to_all x1, blocking collectives, body(): square = lax.all_to_all(sum_of(square), TENSOR, 0, 0, tiled=True)  27.3 us
    all_to_all x1, blocking collectives, body(): part = add_x(lax.all_to_all(part, 'x', 0, 0, tiled=True))  19.5 us
    all_to_all x1, blocking collectives, body(): input_grad = add_y(lax.all_to_all(part, 'y', 0, 0, tiled=True))  18.2 us
    all_to_all x1, starting transfers between devices, body(): got = lax.all_to_all(send, 'seq', 0, 0, tiled=True)  15.8 us
    all_to_all x1, blocking collectives, body(): square = lax.all_to_all(square, 'seq', 0, 0, tiled=True)  15.2 us
    reduce_scatter x1, waiting for transfers between devices, body(): summed = lax.psum_scatter(terms, 'seq', scatter_dimension=1, tiled=True)  6.11 us
    pallas_call x1, Pallas kernels, project(): call(project_kernel, [SMEM, SMEM, HBM, HBM, HBM], [VMEM, VMEM], [shape_of...  6.07 us
    all_to_all x1, waiting for transfers between devices, body(): got = lax.all_to_all(send, 'seq', 0, 0, tiled=True)  5.86 us
  transfers between devices with their start and end apart: 3, of which 3 were waited for; matrix products, arithmetic and copies ran while one was open for 0% of the time, Pallas kernels for 7%

profile of v5, /device:TPU:1, one launch (start us, length us, event | category | flops | bytes accessed | tf_op | source)
XLA Modules:
  0.0 154.1 jit_solution(4853668048446884479)
XLA Ops:
  7.8 0.0 copy-start.4
  7.8 0.0 copy-start.6
  7.8 6.1 %shard_map.68 = (bf16[3,96,192]{2,1,0:T(8,128)(2,1)}, bf16[12,72,128]{2,1,0:T(8,128)(2,1)}) custom-call(f32[1]{0:T(128)S(6)} %copy.8.rate_ref, s32[4]{0:T(128)} %events_ref.5, bf16[192,6144]{1,0:T(8,128)(2,1)} %x_ref.3, bf16[288,6144]{1,0:T(8,128)(2,1)} %bitcast.12, bf16[192,96]{1,0:T(8,128)(2,1)} %o_ref.5), custom_call_target="tpu_custom_call" | custom-call | flops 679477248 | bytes 5898240 | tf_op jit(solution)/shard_map/pallas_call | solution.py:291
  13.9 0.0 copy-start.1
  13.9 15.8 %all-to-all-start = ((bf16[12,72,128]{2,1,0:T(8,128)(2,1)}), bf16[12,72,128]{2,1,0:T(8,128)(2,1)S(1)}, u32[]{:S(2)}, u32[]{:S(2)}) async-start(bf16[12,72,128]{2,1,0:T(8,128)(2,1)} %get-tuple-element.12), calls=%async_computation | async-start | bytes 442368 | tf_op jit(solution)/shard_map/all_to_all | solution.py:414
  29.8 0.0 reduce-scatter.2.cloned.1.call-start
  29.8 0.0 copy-done.4
  29.8 0.0 copy-done.6
  29.8 0.0 copy-start.2
  29.9 0.9 copy-done.2
  30.8 0.0 copy-start.3
  30.8 4.2 %shard_map.69 = (f32[288,192]{1,0:T(8,128)S(1)}, bf16[2,288,3072]{2,1,0:T(8,128)(2,1)S(1)}) custom-call(f32[1]{0:T(128)S(6)} %copy.8.rate_ref, s32[4]{0:T(128)S(1)} %copy-done.6, bf16[3,96,192]{2,1,0:T(8,128)(2,1)S(1)} %copy-done.2, bf16[192,96]{1,0:T(8,128)(2,1)S(1)} %copy-done.4, bf16[288,6144]{1,0:T(8,128)(2,1)} %bitcast.13), custom_call_target="tpu_custom_call" | custom-call | flops 70778880 | bytes 7077888 | tf_op jit(solution)/shard_map/pallas_call | solution.py:312
  35.0 0.0 copy-start
  35.0 1.7 %copy-done = bf16[2,288,3072]{2,1,0:T(8,128)(2,1)} copy-done((bf16[2,288,3072]{2,1,0:T(8,128)(2,1)}, bf16[2,288,3072]{2,1,0:T(8,128)(2,1)S(1)}, u32[]{:S(2)}) %copy-start) | copy-done | bytes 3538968
  36.7 5.9 %all-to-all-done.got_ref = bf16[12,72,128]{2,1,0:T(8,128)(2,1)S(1)} async-done(((bf16[12,72,128]{2,1,0:T(8,128)(2,1)}), bf16[12,72,128]{2,1,0:T(8,128)(2,1)S(1)}, u32[]{:S(2)}, u32[]{:S(2)}) %all-to-all-start) | async-done | bytes 221216 | tf_op jit(solution)/shard_map/all_to_all | solution.py:414
  42.6 0.0 copy-done.1
  42.6 0.0 copy-done.3
  42.6 3.1 %shard_map.70 = (bf16[288,192]{1,0:T(8,128)(2,1)S(1)}, bf16[288,6144]{1,0:T(8,128)(2,1)}) custom-call(f32[1]{0:T(128)S(6)} %copy.8.rate_ref, s32[4]{0:T(128)S(1)} %copy-done.6, bf16[12,72,128]{2,1,0:T(8,128)(2,1)S(1)} %all-to-all-done.got_ref, f32[288,192]{1,0:T(8,128)S(1)} %get-tuple-element.14.local_ref, bf16[3,96,192]{2,1,0:T(8,128)(2,1)S(1)} %copy-done.3, ...), custom_call_target="tpu_custom_call" | custom-call | flops 679477248 | bytes 5898240 | tf_op jit(solution)/shard_map/pallas_call | solution.py:330
  45.8 0.0 reduce-scatter.2.cloned.1.call-update
  45.8 2.5 %shard_map.71 = bf16[4,192,768]{2,1,0:T(8,128)(2,1)S(1)} custom-call(bf16[288,192]{1,0:T(8,128)(2,1)S(1)} %get-tuple-element.16.grads_ref, bf16[2,288,3072]{2,1,0:T(8,128)(2,1)} %copy-done), custom_call_target="tpu_custom_call" | custom-call | flops 339738624 | bytes 2949120 | tf_op jit(solution)/shard_map/pallas_call | solution.py:345
  48.3 4.7 %collective-permute-start = (bf16[4,192,768]{2,1,0:T(8,128)(2,1)S(1)}, bf16[4,192,768]{2,1,0:T(8,128)(2,1)S(1)}, u32[]{:S(2)}, u32[]{:S(2)}) collective-permute-start(bf16[4,192,768]{2,1,0:T(8,128)(2,1)S(1)} %shard_map.71), channel_id=1, source_target_pairs={{0,1},{1,0},{2,3},{3,2},{4,5},{5,4},{6,7},{7,6},{8,9},{9,8},{10,11... | collective-permute-start | bytes 3538952 | tf_op jit(solution)/shard_map/ppermute | solution.py:420
  53.0 2.5 %collective-permute-done.taken_ref = bf16[4,192,768]{2,1,0:T(8,128)(2,1)S(1)} collective-permute-done((bf16[4,192,768]{2,1,0:T(8,128)(2,1)S(1)}, bf16[4,192,768]{2,1,0:T(8,128)(2,1)S(1)}, u32[]{:S(2)}, u32[]{:S(2)}) %collective-permute-start) | collective-permute-done | bytes 1179680 | tf_op jit(solution)/shard_map/ppermute | solution.py:420
  55.5 2.6 %shard_map.72 = bf16[4,192,768]{2,1,0:T(8,128)(2,1)S(1)} custom-call(bf16[288,192]{1,0:T(8,128)(2,1)S(1)} %get-tuple-element.16.grads_ref, bf16[2,288,3072]{2,1,0:T(8,128)(2,1)} %copy-done, bf16[4,192,768]{2,1,0:T(8,128)(2,1)S(1)} %collective-permute-done.taken_ref), custom_call_target="tpu_custom_call" | custom-call | flops 339738624 | bytes 4128768 | tf_op jit(solution)/shard_map/pallas_call | solution.py:357
  58.1 19.5 %all_to_all.31.part_ref = bf16[4,192,768]{2,1,0:T(8,128)(2,1)S(1)} all-to-all(bf16[4,192,768]{2,1,0:T(8,128)(2,1)S(1)} %shard_map.72), channel_id=1, replica_groups=mesh['seq'=12,'x'=4,'y'=8,'core'=2] {'x'}, dimensions={0} | all-to-all | bytes 2359296 | tf_op jit(solution)/shard_map/all_to_all | solution.py:422
  77.5 0.2 shard_map.73
  77.8 18.2 %all_to_all.32.part_ref = bf16[8,96,192]{2,1,0:T(8,128)(2,1)S(1)} all-to-all(bf16[8,96,192]{2,1,0:T(8,128)(2,1)S(1)} %shard_map.73), channel_id=1, replica_groups=mesh['seq'=12,'x'=4,'y'=8,'core'=2] {'y'}, dimensions={0} | all-to-all | bytes 589824 | tf_op jit(solution)/shard_map/all_to_all | solution.py:423
  96.0 0.7 shard_map.74
  96.7 6.1 %reduce-scatter.2.cloned.1.call-done.summed_ref = bf16[288,512]{1,0:T(8,128)(2,1)} async-done(((bf16[288,6144]{1,0:T(8,128)(2,1)}), bf16[288,512]{1,0:T(8,128)(2,1)}) %reduce-scatter.2.cloned.1.call-update) | async-done | bytes 294928 | tf_op jit(solution)/shard_map/reduce_scatter | solution.py:417
  102.8 0.0 copy-start.5
  102.8 1.0 copy-done.5
  103.8 0.1 shard_map.75
  103.9 15.2 %all_to_all.33.parts_ref = f32[12,1,128]{2,1,0:T(1,128)S(1)} all-to-all(f32[12,1,128]{2,1,0:T(1,128)S(1)} %get-tuple-element.20), channel_id=1, replica_groups=mesh['seq'=12,'x'=4,'y'=8,'core'=2] {'seq'}, dimensions={0} | all-to-all | bytes 12288 | tf_op jit(solution)/shard_map/all_to_all | solution.py:427
  119.1 27.3 %all_to_all.34 = f32[64,1,128]{2,1,0:T(1,128)S(1)} all-to-all(f32[64,1,128]{2,1,0:T(1,128)S(1)} %bitcast.11), channel_id=1, replica_groups=mesh['seq'=12,'x'=4,'y'=8,'core'=2] {'x','y','core'}, dimensions={0} | all-to-all | bytes 65536 | tf_op jit(solution)/shard_map/all_to_all | solution.py:428
  146.4 0.9 shard_map.77
  (1 shorter events, 0.0 us)
Async XLA Ops:
  7.8 22.0 %copy-start.4 = (bf16[192,96]{1,0:T(8,128)(2,1)S(1)}, bf16[192,96]{1,0:T(8,128)(2,1)}, u32[]{:S(2)}) copy-start(bf16[192,96]{1,0:T(8,128)(2,1)} %o_ref.5) | copy-start | bytes 110596
  7.8 22.0 %copy-start.6 = (s32[4]{0:T(128)S(1)}, s32[4]{0:T(128)}, u32[]{:S(2)}) copy-start(s32[4]{0:T(128)} %events_ref.5) | copy-start | bytes 52
  13.9 28.7 %copy-start.1 = (bf16[192,6144]{1,0:T(8,128)(2,1)S(1)}, bf16[192,6144]{1,0:T(8,128)(2,1)}, u32[]{:S(2)}) copy-start(bf16[192,6144]{1,0:T(8,128)(2,1)} %x_ref.3) | copy-start | bytes 7077892
  13.9 28.7 %all-to-all-start = ((bf16[12,72,128]{2,1,0:T(8,128)(2,1)}), bf16[12,72,128]{2,1,0:T(8,128)(2,1)S(1)}, u32[]{:S(2)}, u32[]{:S(2)}) async-start(bf16[12,72,128]{2,1,0:T(8,128)(2,1)} %get-tuple-element.12), calls=%async_computation | async-start | bytes 442368 | tf_op jit(solution)/shard_map/all_to_all | solution.py:414
  29.8 73.0 %reduce-scatter.2.cloned.1.call-start = ((), (), s32[]{:S(2)}) async-start(), calls=%async_computation.6 | async-start | bytes 3833856 | tf_op jit(solution)/shard_map/reduce_scatter | solution.py:417
  29.8 0.9 copy-start.2
  30.8 11.9 %copy-start.3 = (bf16[3,96,192]{2,1,0:T(8,128)(2,1)S(1)}, bf16[3,96,192]{2,1,0:T(8,128)(2,1)}, u32[]{:S(2)}) copy-start(bf16[3,96,192]{2,1,0:T(8,128)(2,1)} %get-tuple-element.13.qkv_ref) | copy-start | bytes 331780
  35.0 1.8 %copy-start = (bf16[2,288,3072]{2,1,0:T(8,128)(2,1)}, bf16[2,288,3072]{2,1,0:T(8,128)(2,1)S(1)}, u32[]{:S(2)}) copy-start(bf16[2,288,3072]{2,1,0:T(8,128)(2,1)S(1)} %get-tuple-element.17.w_ref) | copy-start | bytes 10616836
  48.3 7.2 %collective-permute-start = (bf16[4,192,768]{2,1,0:T(8,128)(2,1)S(1)}, bf16[4,192,768]{2,1,0:T(8,128)(2,1)S(1)}, u32[]{:S(2)}, u32[]{:S(2)}) collective-permute-start(bf16[4,192,768]{2,1,0:T(8,128)(2,1)S(1)} %shard_map.71), channel_id=1, source_target_pairs={{0,1},{1,0},{2,3},{3,2},{4,5},{5,4},{6,7},{7,6},{8,9},{9,8},{10,11... | collective-permute-start | bytes 3538952 | tf_op jit(solution)/shard_map/ppermute | solution.py:420
  102.8 1.0 copy-start.5
Sparse Core Ops, SparseCore 0:
  45.9 56.8 reduce-scatter.1

commit v6 on v4

--- a/solution.py
+++ b/solution.py
@@ -147,31 +147,22 @@
         send_ref[d] = (jnp.where(d > me, forward, reverse) * weight).astype(BF16)
 
 
-def local_kernel(rate_ref, events_ref, qkv_ref, o_ref, w_ref, grads_ref, half_ref):
-    core = lax.axis_index("core")
-    block = w_ref[...]
-    for c in range(NC):
-        mine = jnp.concatenate(
-            [block[:, (y * NC + c) * OUT_ROWS : (y * NC + c + 1) * OUT_ROWS] for y in range(NY)],
-            axis=1,
-        )
-        half_ref[lax.rem(core + c, NC)] = mine
-
-    @pl.when(pl.program_id(0) == 0)
-    def _():
-        first = lax.axis_index("seq") * TOK
-        rate = rate_ref[0]
-        row = lax.broadcasted_iota(jnp.int32, (TOK, 1), 0)
-        column = lax.broadcasted_iota(jnp.int32, (1, TOK), 1)
-        later = row >= column
-        gap = log_decay(rate, events_ref, first, row) - log_decay(rate, events_ref, first, column)
-        weight = jnp.where(later, jnp.exp(jnp.where(later, gap, 0.0)), 0.0)
-        query, keys, values, out = qkv_ref[0], qkv_ref[1], qkv_ref[2], o_ref[...]
-        scores = dot(query, keys, TN) * weight
-        dscores = dot(out, values, NN) * weight
-        grads_ref[:DH] = dot_wide_right(keys, dscores, NT)
-        grads_ref[DH : 2 * DH] = dot_wide_right(query, dscores, NN)
-        grads_ref[2 * DH :] = dot_wide_right(out, scores, TN)
+def local_kernel(rate_ref, events_ref, qkv_ref, o_ref, x_ref, grads_ref, x_buf, x_sem):
+    x_copy = fetch([(x_ref, x_buf)], x_sem)
+    first = lax.axis_index("seq") * TOK
+    rate = rate_ref[0]
+    row = lax.broadcasted_iota(jnp.int32, (TOK, 1), 0)
+    column = lax.broadcasted_iota(jnp.int32, (1, TOK), 1)
+    later = row >= column
+    gap = log_decay(rate, events_ref, first, row) - log_decay(rate, events_ref, first, column)
+    weight = jnp.where(later, jnp.exp(jnp.where(later, gap, 0.0)), 0.0)
+    query, keys, values, out = qkv_ref[0], qkv_ref[1], qkv_ref[2], o_ref[...]
+    scores = dot(query, keys, TN) * weight
+    dscores = dot(out, values, NN) * weight
+    grads_ref[:DH] = dot_wide_right(keys, dscores, NT)
+    grads_ref[DH : 2 * DH] = dot_wide_right(query, dscores, NN)
+    grads_ref[2 * DH :] = dot_wide_right(out, scores, TN)
+    wait(x_copy)
 
 
 def weight_kernel(
@@ -205,24 +196,39 @@
     wait(sent)
 
 
-def half_copies(w_ref, w_buf, sems, which):
-    chunks = [columns(k, PER_X) for k in range(NX)]
-    return fetch([(w_ref.at[which, :, at], w_buf.at[:, at]) for at in chunks], sems)
+def fetch_w(w_ref, w_buf, sems):
+    chunks = [columns(k, D // NX) for k in range(NX)]
+    return fetch([(w_ref.at[:, at], w_buf.at[:, at]) for at in chunks], sems)
+
+
+def core_columns(w_buf, k, c):
+    starts = [k * (D // NX) + (y * NC + c) * OUT_ROWS for y in range(NY)]
+    return jnp.concatenate([w_buf[:, at : at + OUT_ROWS] for at in starts], axis=1)
 
 
 def give_kernel(grads_ref, w_ref, give_ref, w_buf, sems):
+    core = lax.axis_index("core")
     grads = grads_ref[...]
-    for k, copy in enumerate(half_copies(w_ref, w_buf, sems, 1)):
+    for k, copy in enumerate(fetch_w(w_ref, w_buf, sems)):
         wait([copy])
-        give_ref[k] = dot(grads, w_buf[:, columns(k, PER_X)], TN).astype(BF16)
+        for c in range(NC):
+
+            @pl.when(core != c)
+            def _():
+                give_ref[k] = dot(grads, core_columns(w_buf, k, c), TN).astype(BF16)
 
 
 def keep_kernel(grads_ref, w_ref, taken_ref, sum_ref, w_buf, sems):
+    core = lax.axis_index("core")
     grads = grads_ref[...]
-    for k, copy in enumerate(half_copies(w_ref, w_buf, sems, 0)):
+    for k, copy in enumerate(fetch_w(w_ref, w_buf, sems)):
         wait([copy])
-        mine = dot(grads, w_buf[:, columns(k, PER_X)], TN)
-        sum_ref[k] = (mine + taken_ref[k].astype(F32)).astype(BF16)
+        for c in range(NC):
+
+            @pl.when(core == c)
+            def _():
+                mine = dot(grads, core_columns(w_buf, k, c), TN)
+                sum_ref[k] = (mine + taken_ref[k].astype(F32)).astype(BF16)
 
 
 def add_x_kernel(part_ref, out_ref):
@@ -306,24 +312,16 @@
     )(rate, events, x, w, o)
 
 
-def local_part(rate, events, qkv, o, w):
-    def whole(*shape):
-        return pl.BlockSpec(shape, lambda i: (0,) * len(shape))
-
+def local_part(rate, events, qkv, o, x):
     return call(
         local_kernel,
-        [
-            SMEM,
-            SMEM,
-            whole(3, DH, TOK),
-            whole(TOK, DH),
-            pl.BlockSpec((PARTS, D // NX), lambda i: (0, i)),
-        ],
-        [whole(PARTS, TOK), pl.BlockSpec((NC, PARTS, PER_X), lambda i: (0, 0, i))],
-        [shape_of((PARTS, TOK), F32), shape_of((NC, PARTS, HALF))],
-        (20 * TOK * TOK * DH, 4 * D * PARTS),
-        grid=(NX,),
-    )(rate, events, qkv, o, w)
+        [SMEM, SMEM, VMEM, VMEM, HBM],
+        [VMEM, VMEM],
+        [shape_of((PARTS, TOK), F32), shape_of((TOK, D))],
+        (20 * TOK * TOK * DH, 8 * TOK * PARTS + 2 * TOK * D),
+        [DMA((1,))],
+        limit=MIDDLE,
+    )(rate, events, qkv, o, x)
 
 
 def weight_terms(rate, events, got, local, qkv, o, x):
@@ -341,28 +339,28 @@
     )(rate, events, got, local, qkv, o, x)
 
 
-def give_part(grads, halves):
+def give_part(grads, w):
     return call(
         give_kernel,
         [VMEM, HBM],
         VMEM,
         shape_of((NX, TOK, PER_X)),
         (TOK * D * PARTS, D * (TOK + PARTS)),
-        [pltpu.VMEM((PARTS, HALF), BF16), DMA((NX,))],
+        [pltpu.VMEM((PARTS, D), BF16), DMA((NX,))],
         limit=MIDDLE,
-    )(grads, halves)
-
-
-def keep_part(grads, halves, taken):
+    )(grads, w)
+
+
+def keep_part(grads, w, taken):
     return call(
         keep_kernel,
         [VMEM, HBM, VMEM],
         VMEM,
         shape_of((NX, TOK, PER_X)),
         (TOK * D * PARTS, D * (2 * TOK + PARTS)),
-        [pltpu.VMEM((PARTS, HALF), BF16), DMA((NX,))],
+        [pltpu.VMEM((PARTS, D), BF16), DMA((NX,))],
         limit=MIDDLE,
-    )(grads, halves, taken)
+    )(grads, w, taken)
 
 
 def add_x(parts):
@@ -412,13 +410,13 @@
     w = projection_matrices.transpose(1, 2, 0).reshape(PARTS, D)
     qkv, send = project(rate, events, x, w, o)
     got = lax.all_to_all(send, "seq", 0, 0, tiled=True)
-    local, halves = local_part(rate, events, qkv, o, w)
+    local, x = local_part(rate, events, qkv, o, x)
     grads, terms = weight_terms(rate, events, got, local, qkv, o, x)
     summed = lax.psum_scatter(terms, "seq", scatter_dimension=1, tiled=True)
 
-    give = give_part(grads, halves)
+    give = give_part(grads, w)
     taken = lax.ppermute(give, "core", [(0, 1), (1, 0)])
-    part = keep_part(grads, halves, taken)
+    part = keep_part(grads, w, taken)
     part = add_x(lax.all_to_all(part, "x", 0, 0, tiled=True))
     input_grad = add_y(lax.all_to_all(part, "y", 0, 0, tiled=True))
 

time: 154 us -> 153 us (level)
  Pallas kernels: 21.9 us -> 20.2 us
    pallas_call x1, Pallas kernels: 5.74 us -> 2.24 us  [local_part(): call(local_kernel, [SMEM, SMEM, VMEM, VMEM, HBM], [VMEM, VMEM], [shape_of...]
    all_to_all x1, waiting for transfers between devices: 7.04 us -> 9.6 us  [body(): got = lax.all_to_all(send, 'seq', 0, 0, tiled=True)]
    reduce_scatter x1, waiting for transfers between devices: 6.03 us -> 4.04 us  [body(): summed = lax.psum_scatter(terms, 'seq', scatter_dimension=1, tiled=True)]
  transfers between devices with their start and end apart: 3 -> 3, of which waited for: 3 -> 3; matrix products, arithmetic and copies ran while one was open for 0% -> 0% of each run, Pallas kernels for 8% -> 7%
where the time goes in v6:
time: 153 us
  blocking collectives  79 us (52%)
  starting transfers between devices  20.6 us (13%)
  Pallas kernels  20.2 us (13%)
  waiting for transfers between devices  16.1 us (11%)
  between operations  14.8 us (10%)
  local copies, waits for them, and re-layouts  1.88 us (1%)
    all_to_all x1, blocking collectives, body(): square = lax.all_to_all(square, TENSOR, 0, 0, tiled=True)  26 us
    all_to_all x1, blocking collectives, body(): part = add_x(lax.all_to_all(part, 'x', 0, 0, tiled=True))  19.4 us
    all_to_all x1, blocking collectives, body(): input_grad = add_y(lax.all_to_all(part, 'y', 0, 0, tiled=True))  18.3 us
    all_to_all x1, starting transfers between devices, body(): got = lax.all_to_all(send, 'seq', 0, 0, tiled=True)  15.8 us
    all_to_all x1, blocking collectives, body(): square = lax.all_to_all(sum_of(square), 'seq', 0, 0, tiled=True)  15.4 us
    all_to_all x1, waiting for transfers between devices, body(): got = lax.all_to_all(send, 'seq', 0, 0, tiled=True)  9.6 us
    pallas_call x1, Pallas kernels, project(): call(project_kernel, [SMEM, SMEM, HBM, HBM, HBM], [VMEM, VMEM], [shape_of...  6.07 us
    ppermute x1, starting transfers between devices, body(): taken = lax.ppermute(give, 'core', [(0, 1), (1, 0)])  4.69 us
  transfers between devices with their start and end apart: 3, of which 3 were waited for; matrix products, arithmetic and copies ran while one was open for 0% of the time, Pallas kernels for 7%

profile of v6, /device:TPU:1, one launch (start us, length us, event | category | flops | bytes accessed | tf_op | source)
XLA Modules:
  0.0 152.5 jit_solution(12417934697731463572)
XLA Ops:
  7.8 0.0 copy-start.2
  7.8 0.0 copy-start.4
  7.8 6.1 %shard_map.68 = (bf16[3,96,192]{2,1,0:T(8,128)(2,1)}, bf16[12,72,128]{2,1,0:T(8,128)(2,1)}) custom-call(f32[1]{0:T(128)S(6)} %copy.8.rate_ref, s32[4]{0:T(128)} %events_ref.5, bf16[192,6144]{1,0:T(8,128)(2,1)} %x_ref.3, bf16[288,6144]{1,0:T(8,128)(2,1)} %bitcast.12, bf16[192,96]{1,0:T(8,128)(2,1)} %o_ref.5), custom_call_target="tpu_custom_call" | custom-call | flops 679477248 | bytes 5898240 | tf_op jit(solution)/shard_map/pallas_call | solution.py:298
  13.9 0.0 copy-start.1
  13.9 15.8 %all-to-all-start = ((bf16[12,72,128]{2,1,0:T(8,128)(2,1)}), bf16[12,72,128]{2,1,0:T(8,128)(2,1)S(1)}, u32[]{:S(2)}, u32[]{:S(2)}) async-start(bf16[12,72,128]{2,1,0:T(8,128)(2,1)} %get-tuple-element.12), calls=%async_computation | async-start | bytes 442368 | tf_op jit(solution)/shard_map/all_to_all | solution.py:412
  29.8 0.0 reduce-scatter.2.cloned.1.call-start
  29.8 0.0 copy-done.2
  29.8 0.0 copy-done.4
  29.8 0.0 copy-start
  29.9 0.9 copy-done
  30.8 2.2 %shard_map.69 = (f32[288,192]{1,0:T(8,128)S(1)}, bf16[192,6144]{1,0:T(8,128)(2,1)S(1)}) custom-call(f32[1]{0:T(128)S(6)} %copy.8.rate_ref, s32[4]{0:T(128)S(1)} %copy-done.4, bf16[3,96,192]{2,1,0:T(8,128)(2,1)S(1)} %copy-done, bf16[192,96]{1,0:T(8,128)(2,1)S(1)} %copy-done.2, bf16[192,6144]{1,0:T(8,128)(2,1)} %x_ref.3), custom_call_target="tpu_custom_call" | custom-call | flops 70778880 | bytes 2801664 | tf_op jit(solution)/shard_map/pallas_call | solution.py:316
  33.0 9.6 %all-to-all-done.got_ref = bf16[12,72,128]{2,1,0:T(8,128)(2,1)S(1)} async-done(((bf16[12,72,128]{2,1,0:T(8,128)(2,1)}), bf16[12,72,128]{2,1,0:T(8,128)(2,1)S(1)}, u32[]{:S(2)}, u32[]{:S(2)}) %all-to-all-start) | async-done | bytes 221216 | tf_op jit(solution)/shard_map/all_to_all | solution.py:412
  42.6 0.0 copy-done.1
  42.6 3.1 %shard_map.70 = (bf16[288,192]{1,0:T(8,128)(2,1)S(1)}, bf16[288,6144]{1,0:T(8,128)(2,1)}) custom-call(f32[1]{0:T(128)S(6)} %copy.8.rate_ref, s32[4]{0:T(128)S(1)} %copy-done.4, bf16[12,72,128]{2,1,0:T(8,128)(2,1)S(1)} %all-to-all-done.got_ref, f32[288,192]{1,0:T(8,128)S(1)} %get-tuple-element.14.local_ref, bf16[3,96,192]{2,1,0:T(8,128)(2,1)S(1)} %copy-done.1, ...), custom_call_target="tpu_custom_call" | custom-call | flops 679477248 | bytes 5898240 | tf_op jit(solution)/shard_map/pallas_call | solution.py:328
  45.7 0.0 reduce-scatter.2.cloned.1.call-update
  45.7 3.4 %shard_map.71 = bf16[4,192,768]{2,1,0:T(8,128)(2,1)S(1)} custom-call(bf16[288,192]{1,0:T(8,128)(2,1)S(1)} %get-tuple-element.17.grads_ref, bf16[288,6144]{1,0:T(8,128)(2,1)} %bitcast.13), custom_call_target="tpu_custom_call" | custom-call | flops 339738624 | bytes 2949120 | tf_op jit(solution)/shard_map/pallas_call | solution.py:343
  49.2 4.7 %collective-permute-start = (bf16[4,192,768]{2,1,0:T(8,128)(2,1)S(1)}, bf16[4,192,768]{2,1,0:T(8,128)(2,1)S(1)}, u32[]{:S(2)}, u32[]{:S(2)}) collective-permute-start(bf16[4,192,768]{2,1,0:T(8,128)(2,1)S(1)} %shard_map.71), channel_id=1, source_target_pairs={{0,1},{1,0},{2,3},{3,2},{4,5},{5,4},{6,7},{7,6},{8,9},{9,8},{10,11... | collective-permute-start | bytes 3538952 | tf_op jit(solution)/shard_map/ppermute | solution.py:418
  53.9 2.5 %collective-permute-done.taken_ref = bf16[4,192,768]{2,1,0:T(8,128)(2,1)S(1)} collective-permute-done((bf16[4,192,768]{2,1,0:T(8,128)(2,1)S(1)}, bf16[4,192,768]{2,1,0:T(8,128)(2,1)S(1)}, u32[]{:S(2)}, u32[]{:S(2)}) %collective-permute-start) | collective-permute-done | bytes 1179680 | tf_op jit(solution)/shard_map/ppermute | solution.py:418
  56.3 3.4 %shard_map.72 = bf16[4,192,768]{2,1,0:T(8,128)(2,1)S(1)} custom-call(bf16[288,192]{1,0:T(8,128)(2,1)S(1)} %get-tuple-element.17.grads_ref, bf16[288,6144]{1,0:T(8,128)(2,1)} %bitcast.14, bf16[4,192,768]{2,1,0:T(8,128)(2,1)S(1)} %collective-permute-done.taken_ref), custom_call_target="tpu_custom_call" | custom-call | flops 339738624 | bytes 4128768 | tf_op jit(solution)/shard_map/pallas_call | solution.py:355
  59.8 19.4 %all_to_all.31.part_ref = bf16[4,192,768]{2,1,0:T(8,128)(2,1)S(1)} all-to-all(bf16[4,192,768]{2,1,0:T(8,128)(2,1)S(1)} %shard_map.72), channel_id=1, replica_groups=mesh['seq'=12,'x'=4,'y'=8,'core'=2] {'x'}, dimensions={0} | all-to-all | bytes 2359296 | tf_op jit(solution)/shard_map/all_to_all | solution.py:420
  79.2 0.2 shard_map.73
  79.4 18.3 %all_to_all.32.part_ref = bf16[8,96,192]{2,1,0:T(8,128)(2,1)S(1)} all-to-all(bf16[8,96,192]{2,1,0:T(8,128)(2,1)S(1)} %shard_map.73), channel_id=1, replica_groups=mesh['seq'=12,'x'=4,'y'=8,'core'=2] {'y'}, dimensions={0} | all-to-all | bytes 589824 | tf_op jit(solution)/shard_map/all_to_all | solution.py:421
  97.7 0.7 shard_map.74
  98.4 4.0 %reduce-scatter.2.cloned.1.call-done.summed_ref = bf16[288,512]{1,0:T(8,128)(2,1)} async-done(((bf16[288,6144]{1,0:T(8,128)(2,1)}), bf16[288,512]{1,0:T(8,128)(2,1)}) %reduce-scatter.2.cloned.1.call-update) | async-done | bytes 294928 | tf_op jit(solution)/shard_map/reduce_scatter | solution.py:415
  102.4 0.0 copy-start.3
  102.4 1.0 copy-done.3
  103.4 0.1 shard_map.75
  103.5 26.0 %all_to_all.33 = f32[64,1,128]{2,1,0:T(1,128)S(1)} all-to-all(f32[64,1,128]{2,1,0:T(1,128)S(1)} %bitcast.11), channel_id=1, replica_groups=mesh['seq'=12,'x'=4,'y'=8,'core'=2] {'x','y','core'}, dimensions={0} | all-to-all | bytes 65536 | tf_op jit(solution)/shard_map/all_to_all | solution.py:425
  129.5 15.4 %all_to_all.34.parts_ref = f32[12,1,128]{2,1,0:T(1,128)S(1)} all-to-all(f32[12,1,128]{2,1,0:T(1,128)S(1)} %shard_map.76), channel_id=1, replica_groups=mesh['seq'=12,'x'=4,'y'=8,'core'=2] {'seq'}, dimensions={0} | all-to-all | bytes 12288 | tf_op jit(solution)/shard_map/all_to_all | solution.py:426
  144.8 0.9 shard_map.77
  (1 shorter events, 0.0 us)
Async XLA Ops:
  7.8 22.0 %copy-start.2 = (bf16[192,96]{1,0:T(8,128)(2,1)S(1)}, bf16[192,96]{1,0:T(8,128)(2,1)}, u32[]{:S(2)}) copy-start(bf16[192,96]{1,0:T(8,128)(2,1)} %o_ref.5) | copy-start | bytes 110596
  7.8 22.0 %copy-start.4 = (s32[4]{0:T(128)S(1)}, s32[4]{0:T(128)}, u32[]{:S(2)}) copy-start(s32[4]{0:T(128)} %events_ref.5) | copy-start | bytes 52
  13.9 28.7 %copy-start.1 = (bf16[3,96,192]{2,1,0:T(8,128)(2,1)S(1)}, bf16[3,96,192]{2,1,0:T(8,128)(2,1)}, u32[]{:S(2)}) copy-start(bf16[3,96,192]{2,1,0:T(8,128)(2,1)} %get-tuple-element.13.qkv_ref) | copy-start | bytes 331780
  13.9 28.7 %all-to-all-start = ((bf16[12,72,128]{2,1,0:T(8,128)(2,1)}), bf16[12,72,128]{2,1,0:T(8,128)(2,1)S(1)}, u32[]{:S(2)}, u32[]{:S(2)}) async-start(bf16[12,72,128]{2,1,0:T(8,128)(2,1)} %get-tuple-element.12), calls=%async_computation | async-start | bytes 442368 | tf_op jit(solution)/shard_map/all_to_all | solution.py:412
  29.8 72.6 %reduce-scatter.2.cloned.1.call-start = ((), (), s32[]{:S(2)}) async-start(), calls=%async_computation.6 | async-start | bytes 3833856 | tf_op jit(solution)/shard_map/reduce_scatter | solution.py:415
  29.8 0.9 copy-start
  49.2 7.2 %collective-permute-start = (bf16[4,192,768]{2,1,0:T(8,128)(2,1)S(1)}, bf16[4,192,768]{2,1,0:T(8,128)(2,1)S(1)}, u32[]{:S(2)}, u32[]{:S(2)}) collective-permute-start(bf16[4,192,768]{2,1,0:T(8,128)(2,1)S(1)} %shard_map.71), channel_id=1, source_target_pairs={{0,1},{1,0},{2,3},{3,2},{4,5},{5,4},{6,7},{7,6},{8,9},{9,8},{10,11... | collective-permute-start | bytes 3538952 | tf_op jit(solution)/shard_map/ppermute | solution.py:418
  102.4 1.0 copy-start.3
Sparse Core Ops, SparseCore 0:
  45.8 56.5 reduce-scatter.1

commit v7 on v6

--- a/solution.py
+++ b/solution.py
@@ -17,8 +17,8 @@
 HALF = D // NC
 PER_X = HALF // NX
 PARTS = 3 * DH
-K_BLOCK = 1536
-S_BLOCK = 1536
+K_BLOCK = 2048
+S_CHUNKS = (512, 1024, 1536, 1536, 1536)
 PACK_ROWS = 72
 PACK_REST = 32
 BIG = 60 << 20
@@ -35,7 +35,6 @@
 NN = (((1,), (0,)), ((), ()))
 NT = (((1,), (1,)), ((), ()))
 TN = (((0,), (0,)), ((), ()))
-TT = (((0,), (1,)), ((), ()))
 
 
 def dot(a, b, dims):
@@ -147,7 +146,7 @@
         send_ref[d] = (jnp.where(d > me, forward, reverse) * weight).astype(BF16)
 
 
-def local_kernel(rate_ref, events_ref, qkv_ref, o_ref, x_ref, grads_ref, x_buf, x_sem):
+def local_kernel(rate_ref, events_ref, qkv_ref, o_ref, x_ref, grads_ref, x_buf, turned_ref, x_sem):
     x_copy = fetch([(x_ref, x_buf)], x_sem)
     first = lax.axis_index("seq") * TOK
     rate = rate_ref[0]
@@ -162,6 +161,7 @@
     grads_ref[:DH] = dot_wide_right(keys, dscores, NT)
     grads_ref[DH : 2 * DH] = dot_wide_right(query, dscores, NN)
     grads_ref[2 * DH :] = dot_wide_right(out, scores, TN)
+    turned_ref[...] = out.astype(F32).T.astype(BF16)
     wait(x_copy)
 
 
@@ -178,7 +178,7 @@
         prefix += jnp.where(j < me, state, 0.0)
         suffix += jnp.where(j > me, state, 0.0)
     prefix, suffix = unpack(prefix), unpack(suffix)
-    dquery = local_ref[:DH] + head_w * dot_wide_left(prefix, o_ref[...], TT)
+    dquery = local_ref[:DH] + head_w * dot_wide_left(prefix, o_ref[...], TN)
     dkey = local_ref[DH : 2 * DH] + tail_w * dot_wide_left(suffix, qkv_ref[2], NN)
     dvalue = local_ref[2 * DH :] + tail_w * dot_wide_left(suffix, qkv_ref[1], TN)
     grads_ref[:DH] = (dquery * SCALE).astype(BF16)
@@ -187,8 +187,10 @@
 
     grads = grads_ref[...]
     sent = []
-    for k in range(D // S_BLOCK):
-        at = columns(k, S_BLOCK)
+    start = 0
+    for k, size in enumerate(S_CHUNKS):
+        at = pl.ds(start, size)
+        start += size
         terms_buf[:, at] = dot(grads, x_ref[:, at], NN).astype(BF16)
         copy = pltpu.make_async_copy(terms_buf.at[:, at], terms_ref.at[:, at], sems.at[k])
         copy.start()
@@ -316,8 +318,8 @@
     return call(
         local_kernel,
         [SMEM, SMEM, VMEM, VMEM, HBM],
-        [VMEM, VMEM],
-        [shape_of((PARTS, TOK), F32), shape_of((TOK, D))],
+        [VMEM, VMEM, VMEM],
+        [shape_of((PARTS, TOK), F32), shape_of((TOK, D)), shape_of((DH, TOK))],
         (20 * TOK * TOK * DH, 8 * TOK * PARTS + 2 * TOK * D),
         [DMA((1,))],
         limit=MIDDLE,
@@ -333,7 +335,7 @@
         (2 * TOK * D * PARTS, 2 * D * (TOK + PARTS)),
         [
             pltpu.VMEM((PARTS, D), BF16),
-            DMA((D // S_BLOCK,)),
+            DMA((len(S_CHUNKS),)),
         ],
         limit=MIDDLE,
     )(rate, events, got, local, qkv, o, x)
@@ -410,7 +412,7 @@
     w = projection_matrices.transpose(1, 2, 0).reshape(PARTS, D)
     qkv, send = project(rate, events, x, w, o)
     got = lax.all_to_all(send, "seq", 0, 0, tiled=True)
-    local, x = local_part(rate, events, qkv, o, x)
+    local, x, o = local_part(rate, events, qkv, o, x)
     grads, terms = weight_terms(rate, events, got, local, qkv, o, x)
     summed = lax.psum_scatter(terms, "seq", scatter_dimension=1, tiled=True)
 

time: 153 us -> 153 us (level)
  no operation moved by 1% of the time
where the time goes in v7:
time: 153 us
  blocking collectives  79.4 us (52%)
  starting transfers between devices  20.6 us (13%)
  Pallas kernels  19.9 us (13%)
  waiting for transfers between devices  16 us (10%)
  between operations  14.8 us (10%)
  local copies, waits for them, and re-layouts  1.88 us (1%)
    all_to_all x1, blocking collectives, body(): square = lax.all_to_all(square, TENSOR, 0, 0, tiled=True)  26.3 us
    all_to_all x1, blocking collectives, body(): part = add_x(lax.all_to_all(part, 'x', 0, 0, tiled=True))  19.4 us
    all_to_all x1, blocking collectives, body(): input_grad = add_y(lax.all_to_all(part, 'y', 0, 0, tiled=True))  18.3 us
    all_to_all x1, starting transfers between devices, body(): got = lax.all_to_all(send, 'seq', 0, 0, tiled=True)  15.9 us
    all_to_all x1, blocking collectives, body(): square = lax.all_to_all(sum_of(square), 'seq', 0, 0, tiled=True)  15.3 us
    all_to_all x1, waiting for transfers between devices, body(): got = lax.all_to_all(send, 'seq', 0, 0, tiled=True)  9.61 us
    pallas_call x1, Pallas kernels, project(): call(project_kernel, [SMEM, SMEM, HBM, HBM, HBM], [VMEM, VMEM], [shape_of...  5.85 us
    ppermute x1, starting transfers between devices, body(): taken = lax.ppermute(give, 'core', [(0, 1), (1, 0)])  4.68 us
  transfers between devices with their start and end apart: 3, of which 3 were waited for; matrix products, arithmetic and copies ran while one was open for 0% of the time, Pallas kernels for 7%

profile of v7, /device:TPU:1, one launch (start us, length us, event | category | flops | bytes accessed | tf_op | source)
XLA Modules:
  0.0 152.5 jit_solution(15445788170416652587)
XLA Ops:
  7.8 0.0 copy-start.3
  7.8 0.0 copy-start.4
  7.8 5.8 %shard_map.68 = (bf16[3,96,192]{2,1,0:T(8,128)(2,1)}, bf16[12,72,128]{2,1,0:T(8,128)(2,1)}) custom-call(f32[1]{0:T(128)S(6)} %copy.8.rate_ref, s32[4]{0:T(128)} %events_ref.5, bf16[192,6144]{1,0:T(8,128)(2,1)} %x_ref.3, bf16[288,6144]{1,0:T(8,128)(2,1)} %bitcast.12, bf16[192,96]{1,0:T(8,128)(2,1)} %o_ref.3), custom_call_target="tpu_custom_call" | custom-call | flops 679477248 | bytes 5898240 | tf_op jit(solution)/shard_map/pallas_call | solution.py:300
  13.7 0.0 copy-start.1
  13.7 15.9 %all-to-all-start = ((bf16[12,72,128]{2,1,0:T(8,128)(2,1)}), bf16[12,72,128]{2,1,0:T(8,128)(2,1)S(1)}, u32[]{:S(2)}, u32[]{:S(2)}) async-start(bf16[12,72,128]{2,1,0:T(8,128)(2,1)} %get-tuple-element.13), calls=%async_computation | async-start | bytes 442368 | tf_op jit(solution)/shard_map/all_to_all | solution.py:414
  29.6 0.0 reduce-scatter.2.cloned.1.call-start
  29.6 0.0 copy-done.3
  29.6 0.0 copy-done.4
  29.6 0.0 copy-start
  29.6 0.9 copy-done
  30.5 2.2 %shard_map.69 = (f32[288,192]{1,0:T(8,128)S(1)}, bf16[192,6144]{1,0:T(8,128)(2,1)S(1)}, bf16[96,192]{1,0:T(8,128)(2,1)S(1)}) custom-call(f32[1]{0:T(128)S(6)} %copy.8.rate_ref, s32[4]{0:T(128)S(1)} %copy-done.4, bf16[3,96,192]{2,1,0:T(8,128)(2,1)S(1)} %copy-done, bf16[192,96]{1,0:T(8,128)(2,1)S(1)} %copy-done.3, bf16[192,6144]{1,0:T(8,128)(2,1)} %x_ref.3), custom_call_target="tpu_custom_call" | custom-call | flops 70778880 | bytes 2801664 | tf_op jit(solution)/shard_map/pallas_call | solution.py:318
  32.8 9.6 %all-to-all-done.got_ref = bf16[12,72,128]{2,1,0:T(8,128)(2,1)S(1)} async-done(((bf16[12,72,128]{2,1,0:T(8,128)(2,1)}), bf16[12,72,128]{2,1,0:T(8,128)(2,1)S(1)}, u32[]{:S(2)}, u32[]{:S(2)}) %all-to-all-start) | async-done | bytes 221216 | tf_op jit(solution)/shard_map/all_to_all | solution.py:414
  42.4 0.0 copy-done.1
  42.4 3.0 %shard_map.70 = (bf16[288,192]{1,0:T(8,128)(2,1)S(1)}, bf16[288,6144]{1,0:T(8,128)(2,1)}) custom-call(f32[1]{0:T(128)S(6)} %copy.8.rate_ref, s32[4]{0:T(128)S(1)} %copy-done.4, bf16[12,72,128]{2,1,0:T(8,128)(2,1)S(1)} %all-to-all-done.got_ref, f32[288,192]{1,0:T(8,128)S(1)} %get-tuple-element.15.local_ref, bf16[3,96,192]{2,1,0:T(8,128)(2,1)S(1)} %copy-done.1, ...), custom_call_target="tpu_custom_call" | custom-call | flops 679477248 | bytes 5898240 | tf_op jit(solution)/shard_map/pallas_call | solution.py:330
  45.4 0.0 reduce-scatter.2.cloned.1.call-update
  45.4 3.4 %shard_map.71 = bf16[4,192,768]{2,1,0:T(8,128)(2,1)S(1)} custom-call(bf16[288,192]{1,0:T(8,128)(2,1)S(1)} %get-tuple-element.19.grads_ref, bf16[288,6144]{1,0:T(8,128)(2,1)} %bitcast.13), custom_call_target="tpu_custom_call" | custom-call | flops 339738624 | bytes 2949120 | tf_op jit(solution)/shard_map/pallas_call | solution.py:345
  48.9 4.7 %collective-permute-start = (bf16[4,192,768]{2,1,0:T(8,128)(2,1)S(1)}, bf16[4,192,768]{2,1,0:T(8,128)(2,1)S(1)}, u32[]{:S(2)}, u32[]{:S(2)}) collective-permute-start(bf16[4,192,768]{2,1,0:T(8,128)(2,1)S(1)} %shard_map.71), channel_id=1, source_target_pairs={{0,1},{1,0},{2,3},{3,2},{4,5},{5,4},{6,7},{7,6},{8,9},{9,8},{10,11... | collective-permute-start | bytes 3538952 | tf_op jit(solution)/shard_map/ppermute | solution.py:420
  53.6 2.5 %collective-permute-done.taken_ref = bf16[4,192,768]{2,1,0:T(8,128)(2,1)S(1)} collective-permute-done((bf16[4,192,768]{2,1,0:T(8,128)(2,1)S(1)}, bf16[4,192,768]{2,1,0:T(8,128)(2,1)S(1)}, u32[]{:S(2)}, u32[]{:S(2)}) %collective-permute-start) | collective-permute-done | bytes 1179680 | tf_op jit(solution)/shard_map/ppermute | solution.py:420
  56.0 3.4 %shard_map.72 = bf16[4,192,768]{2,1,0:T(8,128)(2,1)S(1)} custom-call(bf16[288,192]{1,0:T(8,128)(2,1)S(1)} %get-tuple-element.19.grads_ref, bf16[288,6144]{1,0:T(8,128)(2,1)} %bitcast.14, bf16[4,192,768]{2,1,0:T(8,128)(2,1)S(1)} %collective-permute-done.taken_ref), custom_call_target="tpu_custom_call" | custom-call | flops 339738624 | bytes 4128768 | tf_op jit(solution)/shard_map/pallas_call | solution.py:357
  59.5 19.4 %all_to_all.31.part_ref = bf16[4,192,768]{2,1,0:T(8,128)(2,1)S(1)} all-to-all(bf16[4,192,768]{2,1,0:T(8,128)(2,1)S(1)} %shard_map.72), channel_id=1, replica_groups=mesh['seq'=12,'x'=4,'y'=8,'core'=2] {'x'}, dimensions={0} | all-to-all | bytes 2359296 | tf_op jit(solution)/shard_map/all_to_all | solution.py:422
  78.9 0.2 shard_map.73
  79.2 18.3 %all_to_all.32.part_ref = bf16[8,96,192]{2,1,0:T(8,128)(2,1)S(1)} all-to-all(bf16[8,96,192]{2,1,0:T(8,128)(2,1)S(1)} %shard_map.73), channel_id=1, replica_groups=mesh['seq'=12,'x'=4,'y'=8,'core'=2] {'y'}, dimensions={0} | all-to-all | bytes 589824 | tf_op jit(solution)/shard_map/all_to_all | solution.py:423
  97.4 0.7 shard_map.74
  98.1 3.9 %reduce-scatter.2.cloned.1.call-done.summed_ref = bf16[288,512]{1,0:T(8,128)(2,1)} async-done(((bf16[288,6144]{1,0:T(8,128)(2,1)}), bf16[288,512]{1,0:T(8,128)(2,1)}) %reduce-scatter.2.cloned.1.call-update) | async-done | bytes 294928 | tf_op jit(solution)/shard_map/reduce_scatter | solution.py:417
  102.0 0.0 copy-start.2
  102.0 1.0 copy-done.2
  103.0 0.1 shard_map.75
  103.1 26.3 %all_to_all.33 = f32[64,1,128]{2,1,0:T(1,128)S(1)} all-to-all(f32[64,1,128]{2,1,0:T(1,128)S(1)} %bitcast.11), channel_id=1, replica_groups=mesh['seq'=12,'x'=4,'y'=8,'core'=2] {'x','y','core'}, dimensions={0} | all-to-all | bytes 65536 | tf_op jit(solution)/shard_map/all_to_all | solution.py:427
  129.5 15.3 %all_to_all.34.parts_ref = f32[12,1,128]{2,1,0:T(1,128)S(1)} all-to-all(f32[12,1,128]{2,1,0:T(1,128)S(1)} %shard_map.76), channel_id=1, replica_groups=mesh['seq'=12,'x'=4,'y'=8,'core'=2] {'seq'}, dimensions={0} | all-to-all | bytes 12288 | tf_op jit(solution)/shard_map/all_to_all | solution.py:428
  144.8 0.9 shard_map.77
  (1 shorter events, 0.0 us)
Async XLA Ops:
  7.8 21.8 %copy-start.3 = (bf16[192,96]{1,0:T(8,128)(2,1)S(1)}, bf16[192,96]{1,0:T(8,128)(2,1)}, u32[]{:S(2)}) copy-start(bf16[192,96]{1,0:T(8,128)(2,1)} %o_ref.3) | copy-start | bytes 110596
  7.8 21.8 %copy-start.4 = (s32[4]{0:T(128)S(1)}, s32[4]{0:T(128)}, u32[]{:S(2)}) copy-start(s32[4]{0:T(128)} %events_ref.5) | copy-start | bytes 52
  13.7 28.7 %copy-start.1 = (bf16[3,96,192]{2,1,0:T(8,128)(2,1)S(1)}, bf16[3,96,192]{2,1,0:T(8,128)(2,1)}, u32[]{:S(2)}) copy-start(bf16[3,96,192]{2,1,0:T(8,128)(2,1)} %get-tuple-element.14.qkv_ref) | copy-start | bytes 331780
  13.7 28.7 %all-to-all-start = ((bf16[12,72,128]{2,1,0:T(8,128)(2,1)}), bf16[12,72,128]{2,1,0:T(8,128)(2,1)S(1)}, u32[]{:S(2)}, u32[]{:S(2)}) async-start(bf16[12,72,128]{2,1,0:T(8,128)(2,1)} %get-tuple-element.13), calls=%async_computation | async-start | bytes 442368 | tf_op jit(solution)/shard_map/all_to_all | solution.py:414
  29.6 72.5 %reduce-scatter.2.cloned.1.call-start = ((), (), s32[]{:S(2)}) async-start(), calls=%async_computation.6 | async-start | bytes 3833856 | tf_op jit(solution)/shard_map/reduce_scatter | solution.py:417
  29.6 0.9 copy-start
  48.9 7.1 %collective-permute-start = (bf16[4,192,768]{2,1,0:T(8,128)(2,1)S(1)}, bf16[4,192,768]{2,1,0:T(8,128)(2,1)S(1)}, u32[]{:S(2)}, u32[]{:S(2)}) collective-permute-start(bf16[4,192,768]{2,1,0:T(8,128)(2,1)S(1)} %shard_map.71), channel_id=1, source_target_pairs={{0,1},{1,0},{2,3},{3,2},{4,5},{5,4},{6,7},{7,6},{8,9},{9,8},{10,11... | collective-permute-start | bytes 3538952 | tf_op jit(solution)/shard_map/ppermute | solution.py:420
  102.0 1.0 copy-start.2
Sparse Core Ops, SparseCore 0:
  45.6 56.4 reduce-scatter.1

commit v8 on v6

--- a/solution.py
+++ b/solution.py
@@ -422,7 +422,7 @@
 
     summed, input_grad = lax.optimization_barrier((summed, input_grad))
     square, summed = square_of(summed)
-    square = lax.all_to_all(square, TENSOR, 0, 0, tiled=True)
+    square = lax.all_to_all(square, TENSOR[::-1], 0, 0, tiled=True)
     square = lax.all_to_all(sum_of(square), "seq", 0, 0, tiled=True)
     weight_grad = scaled(square, summed)
     return (input_grad, weight_grad.reshape(3, DH, D // N_SEQ).transpose(2, 0, 1))

time: 153 us -> 153 us (level)
  no operation moved by 1% of the time
where the time goes in v8:
time: 153 us; the launch traced here: 152 us
  blocking collectives  78.9 us (52%)
  starting transfers between devices  20.6 us (13%)
  Pallas kernels  20.2 us (13%)
  waiting for transfers between devices  16.1 us (11%)
  between operations  14.8 us (10%)
  local copies, waits for them, and re-layouts  1.88 us (1%)
    all_to_all x1, blocking collectives, body(): square = lax.all_to_all(square, TENSOR[::-1], 0, 0, tiled=True)  25.9 us
    all_to_all x1, blocking collectives, body(): part = add_x(lax.all_to_all(part, 'x', 0, 0, tiled=True))  19.4 us
    all_to_all x1, blocking collectives, body(): input_grad = add_y(lax.all_to_all(part, 'y', 0, 0, tiled=True))  18.3 us
    all_to_all x1, starting transfers between devices, body(): got = lax.all_to_all(send, 'seq', 0, 0, tiled=True)  15.8 us
    all_to_all x1, blocking collectives, body(): square = lax.all_to_all(sum_of(square), 'seq', 0, 0, tiled=True)  15.4 us
    all_to_all x1, waiting for transfers between devices, body(): got = lax.all_to_all(send, 'seq', 0, 0, tiled=True)  9.6 us
    pallas_call x1, Pallas kernels, project(): call(project_kernel, [SMEM, SMEM, HBM, HBM, HBM], [VMEM, VMEM], [shape_of...  6.07 us
    ppermute x1, starting transfers between devices, body(): taken = lax.ppermute(give, 'core', [(0, 1), (1, 0)])  4.69 us
  transfers between devices with their start and end apart: 3, of which 3 were waited for; matrix products, arithmetic and copies ran while one was open for 0% of the time, Pallas kernels for 7%

profile of v8, /device:TPU:1, one launch (start us, length us, event | category | flops | bytes accessed | tf_op | source)
XLA Modules:
  0.0 152.5 jit_solution(16037464415922789719)
XLA Ops:
  7.8 0.0 copy-start.2
  7.8 0.0 copy-start.4
  7.8 6.1 %shard_map.68 = (bf16[3,96,192]{2,1,0:T(8,128)(2,1)}, bf16[12,72,128]{2,1,0:T(8,128)(2,1)}) custom-call(f32[1]{0:T(128)S(6)} %copy.8.rate_ref, s32[4]{0:T(128)} %events_ref.5, bf16[192,6144]{1,0:T(8,128)(2,1)} %x_ref.3, bf16[288,6144]{1,0:T(8,128)(2,1)} %bitcast.12, bf16[192,96]{1,0:T(8,128)(2,1)} %o_ref.5), custom_call_target="tpu_custom_call" | custom-call | flops 679477248 | bytes 5898240 | tf_op jit(solution)/shard_map/pallas_call | solution.py:298
  13.9 0.0 copy-start.1
  13.9 15.8 %all-to-all-start = ((bf16[12,72,128]{2,1,0:T(8,128)(2,1)}), bf16[12,72,128]{2,1,0:T(8,128)(2,1)S(1)}, u32[]{:S(2)}, u32[]{:S(2)}) async-start(bf16[12,72,128]{2,1,0:T(8,128)(2,1)} %get-tuple-element.12), calls=%async_computation | async-start | bytes 442368 | tf_op jit(solution)/shard_map/all_to_all | solution.py:412
  29.8 0.0 reduce-scatter.2.cloned.1.call-start
  29.8 0.0 copy-done.2
  29.8 0.0 copy-done.4
  29.8 0.0 copy-start
  29.9 0.9 copy-done
  30.8 2.2 %shard_map.69 = (f32[288,192]{1,0:T(8,128)S(1)}, bf16[192,6144]{1,0:T(8,128)(2,1)S(1)}) custom-call(f32[1]{0:T(128)S(6)} %copy.8.rate_ref, s32[4]{0:T(128)S(1)} %copy-done.4, bf16[3,96,192]{2,1,0:T(8,128)(2,1)S(1)} %copy-done, bf16[192,96]{1,0:T(8,128)(2,1)S(1)} %copy-done.2, bf16[192,6144]{1,0:T(8,128)(2,1)} %x_ref.3), custom_call_target="tpu_custom_call" | custom-call | flops 70778880 | bytes 2801664 | tf_op jit(solution)/shard_map/pallas_call | solution.py:316
  33.0 9.6 %all-to-all-done.got_ref = bf16[12,72,128]{2,1,0:T(8,128)(2,1)S(1)} async-done(((bf16[12,72,128]{2,1,0:T(8,128)(2,1)}), bf16[12,72,128]{2,1,0:T(8,128)(2,1)S(1)}, u32[]{:S(2)}, u32[]{:S(2)}) %all-to-all-start) | async-done | bytes 221216 | tf_op jit(solution)/shard_map/all_to_all | solution.py:412
  42.6 0.0 copy-done.1
  42.6 3.1 %shard_map.70 = (bf16[288,192]{1,0:T(8,128)(2,1)S(1)}, bf16[288,6144]{1,0:T(8,128)(2,1)}) custom-call(f32[1]{0:T(128)S(6)} %copy.8.rate_ref, s32[4]{0:T(128)S(1)} %copy-done.4, bf16[12,72,128]{2,1,0:T(8,128)(2,1)S(1)} %all-to-all-done.got_ref, f32[288,192]{1,0:T(8,128)S(1)} %get-tuple-element.14.local_ref, bf16[3,96,192]{2,1,0:T(8,128)(2,1)S(1)} %copy-done.1, ...), custom_call_target="tpu_custom_call" | custom-call | flops 679477248 | bytes 5898240 | tf_op jit(solution)/shard_map/pallas_call | solution.py:328
  45.7 0.0 reduce-scatter.2.cloned.1.call-update
  45.7 3.4 %shard_map.71 = bf16[4,192,768]{2,1,0:T(8,128)(2,1)S(1)} custom-call(bf16[288,192]{1,0:T(8,128)(2,1)S(1)} %get-tuple-element.17.grads_ref, bf16[288,6144]{1,0:T(8,128)(2,1)} %bitcast.13), custom_call_target="tpu_custom_call" | custom-call | flops 339738624 | bytes 2949120 | tf_op jit(solution)/shard_map/pallas_call | solution.py:343
  49.2 4.7 %collective-permute-start = (bf16[4,192,768]{2,1,0:T(8,128)(2,1)S(1)}, bf16[4,192,768]{2,1,0:T(8,128)(2,1)S(1)}, u32[]{:S(2)}, u32[]{:S(2)}) collective-permute-start(bf16[4,192,768]{2,1,0:T(8,128)(2,1)S(1)} %shard_map.71), channel_id=1, source_target_pairs={{0,1},{1,0},{2,3},{3,2},{4,5},{5,4},{6,7},{7,6},{8,9},{9,8},{10,11... | collective-permute-start | bytes 3538952 | tf_op jit(solution)/shard_map/ppermute | solution.py:418
  53.9 2.5 %collective-permute-done.taken_ref = bf16[4,192,768]{2,1,0:T(8,128)(2,1)S(1)} collective-permute-done((bf16[4,192,768]{2,1,0:T(8,128)(2,1)S(1)}, bf16[4,192,768]{2,1,0:T(8,128)(2,1)S(1)}, u32[]{:S(2)}, u32[]{:S(2)}) %collective-permute-start) | collective-permute-done | bytes 1179680 | tf_op jit(solution)/shard_map/ppermute | solution.py:418
  56.3 3.4 %shard_map.72 = bf16[4,192,768]{2,1,0:T(8,128)(2,1)S(1)} custom-call(bf16[288,192]{1,0:T(8,128)(2,1)S(1)} %get-tuple-element.17.grads_ref, bf16[288,6144]{1,0:T(8,128)(2,1)} %bitcast.14, bf16[4,192,768]{2,1,0:T(8,128)(2,1)S(1)} %collective-permute-done.taken_ref), custom_call_target="tpu_custom_call" | custom-call | flops 339738624 | bytes 4128768 | tf_op jit(solution)/shard_map/pallas_call | solution.py:355
  59.8 19.4 %all_to_all.31.part_ref = bf16[4,192,768]{2,1,0:T(8,128)(2,1)S(1)} all-to-all(bf16[4,192,768]{2,1,0:T(8,128)(2,1)S(1)} %shard_map.72), channel_id=1, replica_groups=mesh['seq'=12,'x'=4,'y'=8,'core'=2] {'x'}, dimensions={0} | all-to-all | bytes 2359296 | tf_op jit(solution)/shard_map/all_to_all | solution.py:420
  79.2 0.2 shard_map.73
  79.4 18.3 %all_to_all.32.part_ref = bf16[8,96,192]{2,1,0:T(8,128)(2,1)S(1)} all-to-all(bf16[8,96,192]{2,1,0:T(8,128)(2,1)S(1)} %shard_map.73), channel_id=1, replica_groups=mesh['seq'=12,'x'=4,'y'=8,'core'=2] {'y'}, dimensions={0} | all-to-all | bytes 589824 | tf_op jit(solution)/shard_map/all_to_all | solution.py:421
  97.7 0.7 shard_map.74
  98.4 4.0 %reduce-scatter.2.cloned.1.call-done.summed_ref = bf16[288,512]{1,0:T(8,128)(2,1)} async-done(((bf16[288,6144]{1,0:T(8,128)(2,1)}), bf16[288,512]{1,0:T(8,128)(2,1)}) %reduce-scatter.2.cloned.1.call-update) | async-done | bytes 294928 | tf_op jit(solution)/shard_map/reduce_scatter | solution.py:415
  102.4 0.0 copy-start.3
  102.4 1.0 copy-done.3
  103.4 0.1 shard_map.75
  103.5 25.9 %all_to_all.33 = f32[64,1,128]{2,1,0:T(1,128)S(1)} all-to-all(f32[64,1,128]{2,1,0:T(1,128)S(1)} %bitcast.11), channel_id=1, replica_groups=mesh['seq'=12,'x'=4,'y'=8,'core'=2] {'core','y','x'}, dimensions={0} | all-to-all | bytes 65536 | tf_op jit(solution)/shard_map/all_to_all | solution.py:425
  129.4 15.4 %all_to_all.34.parts_ref = f32[12,1,128]{2,1,0:T(1,128)S(1)} all-to-all(f32[12,1,128]{2,1,0:T(1,128)S(1)} %shard_map.76), channel_id=1, replica_groups=mesh['seq'=12,'x'=4,'y'=8,'core'=2] {'seq'}, dimensions={0} | all-to-all | bytes 12288 | tf_op jit(solution)/shard_map/all_to_all | solution.py:426
  144.7 0.9 shard_map.77
  (1 shorter events, 0.0 us)
Async XLA Ops:
  7.8 22.0 %copy-start.2 = (bf16[192,96]{1,0:T(8,128)(2,1)S(1)}, bf16[192,96]{1,0:T(8,128)(2,1)}, u32[]{:S(2)}) copy-start(bf16[192,96]{1,0:T(8,128)(2,1)} %o_ref.5) | copy-start | bytes 110596
  7.8 22.0 %copy-start.4 = (s32[4]{0:T(128)S(1)}, s32[4]{0:T(128)}, u32[]{:S(2)}) copy-start(s32[4]{0:T(128)} %events_ref.5) | copy-start | bytes 52
  13.9 28.7 %copy-start.1 = (bf16[3,96,192]{2,1,0:T(8,128)(2,1)S(1)}, bf16[3,96,192]{2,1,0:T(8,128)(2,1)}, u32[]{:S(2)}) copy-start(bf16[3,96,192]{2,1,0:T(8,128)(2,1)} %get-tuple-element.13.qkv_ref) | copy-start | bytes 331780
  13.9 28.7 %all-to-all-start = ((bf16[12,72,128]{2,1,0:T(8,128)(2,1)}), bf16[12,72,128]{2,1,0:T(8,128)(2,1)S(1)}, u32[]{:S(2)}, u32[]{:S(2)}) async-start(bf16[12,72,128]{2,1,0:T(8,128)(2,1)} %get-tuple-element.12), calls=%async_computation | async-start | bytes 442368 | tf_op jit(solution)/shard_map/all_to_all | solution.py:412
  29.8 72.6 %reduce-scatter.2.cloned.1.call-start = ((), (), s32[]{:S(2)}) async-start(), calls=%async_computation.6 | async-start | bytes 3833856 | tf_op jit(solution)/shard_map/reduce_scatter | solution.py:415
  29.8 0.9 copy-start
  49.2 7.2 %collective-permute-start = (bf16[4,192,768]{2,1,0:T(8,128)(2,1)S(1)}, bf16[4,192,768]{2,1,0:T(8,128)(2,1)S(1)}, u32[]{:S(2)}, u32[]{:S(2)}) collective-permute-start(bf16[4,192,768]{2,1,0:T(8,128)(2,1)S(1)} %shard_map.71), channel_id=1, source_target_pairs={{0,1},{1,0},{2,3},{3,2},{4,5},{5,4},{6,7},{7,6},{8,9},{9,8},{10,11... | collective-permute-start | bytes 3538952 | tf_op jit(solution)/shard_map/ppermute | solution.py:418
  102.4 1.0 copy-start.3
Sparse Core Ops, SparseCore 0:
  45.8 56.5 reduce-scatter.1
